TPU v7x, 256 devices: a whole 4x4x8 slice. The times are simulated.
256 devices in a mesh: dp: 64 (over x, z, core), dim: 4 (over y).
Axes of the slice: x: 4, y: 4, z: 8, core: 2. Of those that a mesh axis runs over, the one named last changes fastest.
Arguments:
- vectors: bfloat16 [768, 65536], P('dim', 'dp'), may hold values from -30 to 30
- codes: int32 [64, 65536], P('dim', 'dp'), may hold values from 0 to 255, as said below
- codebook: bfloat16 [256, 768], P(None, 'dim'), may hold values from -4 to 4
Outputs:
- rotation: float32 [768, 768], P('dim')
- new_codebook: float32 [256, 768], P('dp', 'dim')
Inputs may be any that keep to these rules, and one draw needn't show every extreme that they name: `codes`: each entry names a centroid of its subspace; in each subspace at least one centroid, which one is drawn from the seed, is named by no vector.
All inputs are finite; a program needn't handle non-finite values.
Results may differ from a plain program's by a relative error of at most 0.003.
Values may be sent and summed in bfloat16 or wider, within the bound.
A program may use at most 64 MiB of HBM per device.

v0:
```python
import jax
import jax.numpy as jnp
from jax import lax
from jax.sharding import PartitionSpec as P

NS_STEPS = 4


def per_device(vectors, codes, codebook):
    local_width = vectors.shape[0]
    row_count = vectors.shape[1]
    sub_local = codes.shape[0]
    sub_width = local_width // sub_local
    centroid_count = codebook.shape[0]
    dp_count = lax.axis_size("dp")
    dim_count = lax.axis_size("dim")
    total_width = local_width * dim_count
    block_rows = min(512, row_count)
    block_count = row_count // block_rows
    levels = jnp.arange(centroid_count, dtype=jnp.int32)
    book_cube = codebook.reshape(centroid_count, sub_local, sub_width)
    gathered_rows = lax.all_gather(vectors, "dim", axis=0, tiled=True)

    def block_onehot(block_index):
        start = block_index * block_rows
        code_block = lax.dynamic_slice_in_dim(codes, start, block_rows, 1)
        onehot = (code_block[:, :, None] == levels[None, None, :]).astype(jnp.bfloat16)
        row_block = lax.dynamic_slice_in_dim(gathered_rows, start, block_rows, 1)
        return (onehot, row_block)

    def add_cross(block_index, cross_part):
        onehot, row_block = block_onehot(block_index)
        decoded = jnp.einsum("mnk,kmd->nmd", onehot, book_cube, preferred_element_type=jnp.float32)
        decoded = decoded.reshape(block_rows, local_width).astype(jnp.bfloat16)
        return cross_part + jnp.einsum(
            "nd,cn->dc", decoded, row_block, preferred_element_type=jnp.float32
        )

    cross_part = lax.fori_loop(
        0, block_count, add_cross, jnp.zeros((local_width, total_width), jnp.float32)
    )

    def newton_update(rows, whole):
        gram_rows = jnp.dot(rows, whole.T, precision=lax.Precision.HIGHEST)
        return 1.5 * rows - 0.5 * jnp.dot(gram_rows, whole, precision=lax.Precision.HIGHEST)

    own_rows = lax.psum_scatter(cross_part, "dp", scatter_dimension=0, tiled=True)
    thin_width = own_rows.shape[0]
    dim_index = lax.axis_index("dim")

    def gather_spread(rows):
        return lax.all_gather(rows, ("dp", "dim"), axis=0, tiled=True)

    gathered = gather_spread(own_rows)
    magnitude = jnp.sqrt(jnp.sum(gathered * gathered))
    gathered = gathered / magnitude
    own_rows = own_rows / magnitude

    def spread_step(iteration, carry):
        rows, whole = carry
        rows = newton_update(rows, whole)
        return (rows, gather_spread(rows))

    own_rows, gathered = lax.fori_loop(0, NS_STEPS - 1, spread_step, (own_rows, gathered))
    shaped = gathered.reshape(dp_count, dim_count, thin_width, total_width)
    block_part = lax.dynamic_slice_in_dim(shaped, dim_index, 1, 1).reshape(local_width, total_width)
    rotation = newton_update(block_part, gathered)
    rotation_low = rotation.astype(jnp.bfloat16)

    def add_centroids(block_index, carry):
        centroid_sums, counts = carry
        onehot, row_block = block_onehot(block_index)
        rotated = jnp.einsum(
            "cn,dc->nd", row_block, rotation_low, preferred_element_type=jnp.float32
        ).astype(jnp.bfloat16)
        rotated = rotated.reshape(block_rows, sub_local, sub_width)
        centroid_sums = centroid_sums + jnp.einsum(
            "mnk,nmd->kmd", onehot, rotated, preferred_element_type=jnp.float32
        )
        counts = counts + jnp.sum(onehot, axis=1, dtype=jnp.float32).T
        return (centroid_sums, counts)

    start_sums = jnp.zeros((centroid_count, sub_local, sub_width), jnp.float32)
    start_counts = jnp.zeros((centroid_count, sub_local), jnp.float32)
    centroid_sums, counts = lax.fori_loop(0, block_count, add_centroids, (start_sums, start_counts))
    owned_sums, owned_counts = (
        lax.psum_scatter(
            centroid_sums.reshape(centroid_count, local_width),
            "dp",
            scatter_dimension=0,
            tiled=True,
        ),
        lax.psum_scatter(counts, "dp", scatter_dimension=0, tiled=True),
    )
    divisor = jnp.repeat(jnp.maximum(owned_counts, 1.0), sub_width, axis=1)
    new_codebook = owned_sums / divisor
    return (rotation, new_codebook)


def solution(mesh):
    placed = (P("dim", "dp"), P("dim", "dp"), P(None, "dim"))
    return jax.shard_map(
        per_device,
        mesh=mesh,
        in_specs=placed,
        out_specs=(P("dim", None), P("dp", "dim")),
        check_vma=False,
    )
```

profile of v0, /device:TPU:1, one launch (start us, length us, event | category | flops | bytes accessed | tf_op | source)
XLA Modules:
  0.0 969.9 jit_solution(7501567277466070156)
XLA Ops:
  8.9 33.9 %all-gather.8.cloned.1.call-done = bf16[768,1024]{1,0:T(8,128)(2,1)} async-done(((bf16[192,1024]{1,0:T(8,128)(2,1)}), bf16[768,1024]{1,0:T(8,128)(2,1)}) %all-gather.8.cloned.1.call-update) | async-done | bytes 1572880 | tf_op jit(solution)/shard_map/all_gather | solution.py:22
  42.7 6.8 while.43
  51.5 179.6 %all-reduce.6.cloned.1.call-done = f32[192,768]{1,0:T(8,128)} async-done(((f32[192,768]{1,0:T(8,128)}), f32[192,768]{1,0:T(8,128)}) %all-reduce.6.cloned.1.call-update) | async-done | bytes 589840
  233.2 108.4 %all-gather.10.cloned.1.call-done = f32[256,3,768]{2,1,0:T(4,128)} async-done(((f32[1,3,768]{2,1,0:T(4,128)}), f32[256,3,768]{2,1,0:T(4,128)}) %all-gather.10.cloned.1.call-update) | async-done | bytes 2359312 | tf_op jit(solution)/shard_map/all_gather | solution.py:52
  341.6 4.3 multiply_reduce_fusion
  346.5 2.2 broadcast_divide_fusion
  348.7 3.2 reshape.47
  352.8 337.2 %while.42 = (s32[]{:T(128)}, f32[3,768]{1,0:T(4,128)S(1)}, f32[768,768]{1,0:T(8,128)S(1)}, s32[]{:T(128)}) while((s32[]{:T(128)}, f32[3,768]{1,0:T(4,128)S(1)}, f32[768,768]{1,0:T(8,128)S(1)}, s32[]{:T(128)}) %tuple.81), condition=%wide.region_5.0_spmd, body=%wide.region_4.0_spmd.sunk | while | flops 42474240 | bytes 17452180 | solution.py:64
  352.8 2.0 fusion.52
  356.7 105.2 %all-gather.12.cloned.1.call-done = f32[256,3,768]{2,1,0:T(4,128)} async-done(((f32[1,3,768]{2,1,0:T(4,128)}), f32[256,3,768]{2,1,0:T(4,128)}) %all-gather.12.cloned.1.call-update) | async-done | bytes 2359312 | tf_op jit(solution)/shard_map/while/body/eval_jaxpr/all_gather | solution.py:52
  461.9 3.2 reshape.58
  469.1 105.2 %all-gather.12.cloned.1.call-done = f32[256,3,768]{2,1,0:T(4,128)} async-done(((f32[1,3,768]{2,1,0:T(4,128)}), f32[256,3,768]{2,1,0:T(4,128)}) %all-gather.12.cloned.1.call-update) | async-done | bytes 2359312 | tf_op jit(solution)/shard_map/while/body/eval_jaxpr/all_gather | solution.py:52
  574.3 3.2 reshape.58
  577.7 2.0 fusion.52
  581.5 105.2 %all-gather.12.cloned.1.call-done = f32[256,3,768]{2,1,0:T(4,128)} async-done(((f32[1,3,768]{2,1,0:T(4,128)}), f32[256,3,768]{2,1,0:T(4,128)}) %all-gather.12.cloned.1.call-update) | async-done | bytes 2359312 | tf_op jit(solution)/shard_map/while/body/eval_jaxpr/all_gather | solution.py:52
  686.8 3.2 reshape.58
  690.1 2.6 reshape.37
  692.6 2.2 constant_dynamic-slice_fusion.4
  696.3 2.5 fusion.21
  698.8 2.6 fusion.19
  701.3 12.7 %while.44 = (s32[]{:T(128)}, f32[256,16,12]{0,2,1:T(8,128)}, f32[256,16]{0,1:T(8,128)S(1)}, bf16[768,1024]{1,0:T(8,128)(2,1)}, bf16[192,768]{1,0:T(8,128)(2,1)S(...) while((s32[]{:T(128)}, f32[256,16,12]{0,2,1:T(8,128)}, ...), condition=%wide.region_8.0_spmd.clone, body=%wide.region_6.0_spmd.clone.sunk | while | flops 212013056 | bytes 2457774 | solution.py:85
  702.9 2.8 fusion.61
  708.6 3.9 fusion.61
  715.7 245.4 %all-reduce.2 = f32[256,16]{0,1:T(8,128)S(1)} all-reduce(f32[256,16]{0,1:T(8,128)S(1)} %get-tuple-element.256), channel_id=4, replica_groups=mesh['dp'=64,'dim'=4] {'dp'}, use_global_device_ids=true, to_apply=%region_10.0.clone | all-reduce | flops 4096 | bytes 32768
  (78 shorter events, 30.7 us)
Async XLA Ops:
  7.2 35.6 %all-gather.8.cloned.1.call-start = ((), (), s32[]{:S(2)}) async-start(), calls=%async_computation | async-start | bytes 1966080 | tf_op jit(solution)/shard_map/all_gather | solution.py:22
  7.9 223.3 %all-reduce.6.cloned.1.call-start = ((), (), s32[]{:S(2)}) async-start(), calls=%async_computation.2 | async-start | bytes 1179648
  42.7 7.7 copy-start.6
  43.5 2.1 copy-start
  46.9 2.1 copy-start
  49.5 0.8 copy-start.1
  50.4 291.2 %all-gather.10.cloned.1.call-start = ((), (), s32[]{:S(2)}) async-start(), calls=%async_computation.1 | async-start | bytes 3158016 | tf_op jit(solution)/shard_map/all_gather | solution.py:52
  341.6 5.0 copy-start.2
  352.8 109.1 %all-gather.12.cloned.1.call-start = ((), (), s32[]{:S(2)}) async-start(), calls=%async_computation.4 | async-start | bytes 3158016 | tf_op jit(solution)/shard_map/while/body/eval_jaxpr/all_gather | solution.py:52
  356.0 0.6 copy-start.3
  356.7 108.5 %copy-start.4 = (f32[3,768]{1,0:T(4,128)S(1)}, f32[3,768]{1,0:T(4,128)}, u32[]{:S(2)}) copy-start(f32[3,768]{1,0:T(4,128)} %copy-done.3) | copy-start | bytes 27652 | tf_op jit(solution)/shard_map/while
  465.2 109.1 %all-gather.12.cloned.1.call-start = ((), (), s32[]{:S(2)}) async-start(), calls=%async_computation.4 | async-start | bytes 3158016 | tf_op jit(solution)/shard_map/while/body/eval_jaxpr/all_gather | solution.py:52
  468.5 0.6 copy-start.3
  469.1 108.5 %copy-start.4 = (f32[3,768]{1,0:T(4,128)S(1)}, f32[3,768]{1,0:T(4,128)}, u32[]{:S(2)}) copy-start(f32[3,768]{1,0:T(4,128)} %copy-done.3) | copy-start | bytes 27652 | tf_op jit(solution)/shard_map/while
  577.6 109.1 %all-gather.12.cloned.1.call-start = ((), (), s32[]{:S(2)}) async-start(), calls=%async_computation.4 | async-start | bytes 3158016 | tf_op jit(solution)/shard_map/while/body/eval_jaxpr/all_gather | solution.py:52
  580.9 0.6 copy-start.3
  581.5 108.5 %copy-start.4 = (f32[3,768]{1,0:T(4,128)S(1)}, f32[3,768]{1,0:T(4,128)}, u32[]{:S(2)}) copy-start(f32[3,768]{1,0:T(4,128)} %copy-done.3) | copy-start | bytes 27652 | tf_op jit(solution)/shard_map/while
  690.0 271.4 %all-reduce.8.cloned.1.call-start = ((), (), s32[]{:S(2)}) async-start(), calls=%async_computation.3 | async-start | bytes 393216
  698.7 2.6 copy-start.5
Sparse Core Ops, SparseCore 0:
  9.8 32.8 all-gather.7
  50.5 180.6 all-reduce.5
  235.5 106.0 all-gather.9
  357.6 104.2 all-gather.11
  470.0 104.2 all-gather.11
  582.4 104.2 all-gather.11
  715.8 175.3 all-reduce.7
where the time goes:
time: 975 us; the launch traced here: 970 us
  waiting for transfers between devices  638 us (65%)
  blocking collectives  245 us (25%)
  local copies, waits for them, and re-layouts  29.5 us (3%)
  matrix products  29.4 us (3%)
  between operations  16 us (2%)
  other arithmetic  10.7 us (1%)
    all_gather x4, waiting for transfers between devices, gather_spread(): return lax.all_gather(rows, ('dp', 'dim'), axis=0, tiled=True)  424 us
    unnamed x1, blocking collectives  245 us
    unnamed x6, waiting for transfers between devices  180 us
    all_gather x1, waiting for transfers between devices, per_device(): gathered_rows = lax.all_gather(vectors, 'dim', axis=0, tiled=True)  33.9 us
  transfers between devices with their start and end apart: 7, of which 6 were waited for; matrix products, arithmetic and copies ran while one was open for 0% of the time, Pallas kernels for 0%

commit v1 on v0

v1 whole, which is shorter than its diff:
```python
import jax
import jax.numpy as jnp
from jax import lax
from jax.experimental import pallas as pl
from jax.experimental.pallas import tpu as pltpu
from jax.sharding import PartitionSpec as P

NX, NZ, NC, NY = 4, 8, 2, 4
D, M, K = 768, 64, 256
SUB = D // M
OWN = D // NY
OWN_M = M // NY
TILES = 18
PADDED = 24
PER_Z = PADDED // NZ
HALF = TILES // 2
MESH = pl.DeviceIdType.MESH
F32, BF16 = jnp.float32, jnp.bfloat16


def position():
    dp = lax.axis_index("dp")
    y = lax.axis_index("dim")
    core = lax.rem(dp, NC)
    z = lax.rem(dp // NC, NZ)
    x = dp // (NC * NZ)
    return x, z, core, y


def device(x, z, core, y):
    return ((x * NZ + z) * NC + core, y)


def greet(peers):
    barrier = pltpu.get_barrier_semaphore()
    for peer in peers:
        pl.semaphore_signal(barrier, inc=1, device_id=peer, device_id_type=MESH)
    pl.semaphore_wait(barrier, len(peers))


def remote(src, dst, send_sem, recv_sem, k, peer):
    return pltpu.make_async_remote_copy(
        src_ref=src,
        dst_ref=dst,
        send_sem=send_sem.at[k],
        recv_sem=recv_sem.at[k],
        device_id=peer,
        device_id_type=MESH,
    )


def gather_kernel(codes_ref, book_ref, codes_all, book_all, send_sem, recv_sem):
    x, z, core, y = position()
    peers = [device(x, z, core, lax.rem(y + off, NY)) for off in range(1, NY)]
    greet(peers)
    copies = []
    for i, peer in enumerate(peers):
        copies.append(remote(book_ref, book_all.at[y], send_sem, recv_sem, 2 * i, peer))
        copies[-1].start()
        copies.append(
            remote(codes_ref, codes_all.at[y], send_sem, recv_sem, 2 * i + 1, peer)
        )
        copies[-1].start()
    codes_all[y] = codes_ref[...]
    book_all[y] = book_ref[...]
    for copy in copies:
        copy.wait()


def gather_codes(codes, book):
    vmem = pl.BlockSpec(memory_space=pltpu.VMEM)
    return pl.pallas_call(
        gather_kernel,
        out_shape=(
            jax.ShapeDtypeStruct((NY,) + codes.shape, codes.dtype),
            jax.ShapeDtypeStruct((NY,) + book.shape, book.dtype),
        ),
        in_specs=[vmem, vmem],
        out_specs=(vmem, vmem),
        scratch_shapes=[pltpu.SemaphoreType.DMA((6,)), pltpu.SemaphoreType.DMA((6,))],
        compiler_params=pltpu.CompilerParams(collective_id=0, has_side_effects=True),
        name="gather_codes",
    )(codes, book)


def cross_kernel(codes_ref, book_ref, vectors_ref, part_ref, codes_int, decoded):
    rows = vectors_ref.shape[1]
    codes_int[...] = codes_ref[...].astype(jnp.int32)
    group = 8
    height = group * SUB
    which = lax.broadcasted_iota(jnp.int32, (height, 128), 0) // SUB

    @pl.loop(0, M // group)
    def _(g):
        base = pl.multiple_of(g * height, 16)
        book = book_ref[pl.ds(base, height), :].astype(F32)
        low, high = book[:, :128], book[:, 128:]
        for block in range(rows // 128):
            cols = pl.ds(block * 128, 128)
            lines = codes_int[pl.ds(pl.multiple_of(g * group, group), group), cols]
            index = jnp.broadcast_to(lines[0:1], (height, 128))
            for s in range(1, group):
                line = jnp.broadcast_to(lines[s : s + 1], (height, 128))
                index = jnp.where(which == s, line, index)
            lane = index & 127
            picked = jnp.where(
                index >= 128,
                jnp.take_along_axis(high, lane, axis=1),
                jnp.take_along_axis(low, lane, axis=1),
            )
            decoded[pl.ds(base, height), cols] = picked.astype(BF16)

    for pair in range(NX * NC):
        strip = lax.dot_general(
            vectors_ref[pair * 24 : pair * 24 + 24, :],
            decoded[...],
            (((1,), (1,)), ((), ())),
            preferred_element_type=F32,
        )
        for t in range(TILES):
            i, j = t // 6, t % 6
            part_ref[pair, t] = strip[i * 8 : i * 8 + 8, j * 128 : j * 128 + 128]
        for t in range(TILES, PADDED):
            part_ref[pair, t] = jnp.zeros((8, 128), F32)


def cross_part(codes_all, book_all, vectors):
    rows = vectors.shape[1]
    vmem = pl.BlockSpec(memory_space=pltpu.VMEM)
    return pl.pallas_call(
        cross_kernel,
        out_shape=jax.ShapeDtypeStruct((NX * NC, PADDED, 8, 128), F32),
        in_specs=[vmem] * 3,
        out_specs=vmem,
        scratch_shapes=[pltpu.VMEM((M, rows), jnp.int32), pltpu.VMEM((D, rows), BF16)],
        compiler_params=pltpu.CompilerParams(vmem_limit_bytes=40 * 2**20),
        name="cross_part",
    )(codes_all, book_all, vectors)


def sum_kernel(
    part_ref, vectors_ref, full, vectors_all,
    box_core, sum_core, box_x, sum_x, box_z, send_sem, recv_sem, send_vec, recv_vec,
):
    x, z, core, y = position()
    sibling = device(x, z, 1 - core, y)
    across_x = [device(lax.rem(x + off, NX), z, core, y) for off in range(1, NX)]
    across_z = [device(x, lax.rem(z + off, NZ), core, y) for off in range(1, NZ)]
    across_y = [device(x, z, core, lax.rem(y + off, NY)) for off in range(1, NY)]
    greet([sibling] + across_x + across_z + across_y)
    sent = []

    def send(src, dst, k, peer):
        copy = remote(src, dst, send_sem, recv_sem, k, peer)
        copy.start()
        sent.append(copy)
        return copy

    first = send(part_ref.at[:, 1 - core], box_core, 0, sibling)
    for i, peer in enumerate(across_y):
        copy = remote(vectors_ref, vectors_all.at[y], send_vec, recv_vec, i, peer)
        copy.start()
    vectors_all[y] = vectors_ref[...]
    first.wait_recv()
    sum_core[...] = part_ref[:, core] + box_core[...]
    stage = [
        send(sum_core.at[lax.rem(x + i + 1, NX)], box_x.at[i], 1 + i, peer)
        for i, peer in enumerate(across_x)
    ]
    for copy in stage:
        copy.wait_recv()
    sum_x[...] = (sum_core[x] + box_x[0]) + (box_x[1] + box_x[2])
    stage = [
        send(
            sum_x.at[pl.ds(lax.rem(z + i + 1, NZ) * PER_Z, PER_Z)],
            box_z.at[i], 4 + i, peer,
        )
        for i, peer in enumerate(across_z)
    ]
    for copy in stage:
        copy.wait_recv()
    mine = pl.ds(z * PER_Z, PER_Z)
    total = sum_x[mine]
    for i in range(NZ - 1):
        total = total + box_z[i]
    full[y, x, core, mine] = total

    own = full.at[y, x, core, mine]
    stage = [send(own, own, 11 + i, peer) for i, peer in enumerate(across_z)]
    for copy in stage:
        copy.wait_recv()
    one, two = pl.ds(0, HALF), pl.ds(HALF, HALF)
    stage = []
    half = full.at[y, x, core, one]
    for i, peer in enumerate(across_x):
        stage.append(send(half, half, 18 + i, peer))
    half = full.at[y, x, core, two]
    for i, peer in enumerate(across_y):
        stage.append(send(half, half, 21 + i, peer))
    for copy in stage:
        copy.wait_recv()
    line_one = full.at[y, :, core, one]
    line_two = full.at[:, x, core, two]
    last_one = [send(line_one, line_one, 24 + i, p) for i, p in enumerate(across_y)]
    last_two = [send(line_two, line_two, 27 + i, p) for i, p in enumerate(across_x)]
    final = [
        send(line_one, line_one, 30, sibling),
        send(line_two, line_two, 31, sibling),
    ]
    for i in range(NX - 1):
        last_one[i].wait_recv()
        line = full.at[lax.rem(y + NY - i - 1, NY), :, core, one]
        final.append(send(line, line, 32 + i, sibling))
        last_two[i].wait_recv()
        line = full.at[:, lax.rem(x + NX - i - 1, NX), core, two]
        final.append(send(line, line, 35 + i, sibling))
    for copy in final:
        copy.wait_recv()
    for copy in sent:
        copy.wait_send()
    for i, peer in enumerate(across_y):
        remote(vectors_ref, vectors_all.at[y], send_vec, recv_vec, i, peer).wait()


def sum_and_gather(part, vectors):
    vmem = pl.BlockSpec(memory_space=pltpu.VMEM)
    return pl.pallas_call(
        sum_kernel,
        out_shape=(
            jax.ShapeDtypeStruct((NY, NX, NC, PADDED, 8, 128), F32),
            jax.ShapeDtypeStruct((NY,) + vectors.shape, vectors.dtype),
        ),
        in_specs=[vmem] * 2,
        out_specs=(vmem, vmem),
        scratch_shapes=[
            pltpu.VMEM((NX, PADDED, 8, 128), F32),
            pltpu.VMEM((NX, PADDED, 8, 128), F32),
            pltpu.VMEM((NX - 1, PADDED, 8, 128), F32),
            pltpu.VMEM((PADDED, 8, 128), F32),
            pltpu.VMEM((NZ - 1, PER_Z, 8, 128), F32),
            pltpu.SemaphoreType.DMA((38,)),
            pltpu.SemaphoreType.DMA((38,)),
            pltpu.SemaphoreType.DMA((NY - 1,)),
            pltpu.SemaphoreType.DMA((NY - 1,)),
        ],
        compiler_params=pltpu.CompilerParams(
            collective_id=1, has_side_effects=True, vmem_limit_bytes=40 * 2**20
        ),
        name="sum_and_gather",
    )(part, vectors)


def split(value):
    high = value.astype(BF16)
    return high, (value - high.astype(F32)).astype(BF16)


NT = (((1,), (1,)), ((), ()))
NN = (((1,), (0,)), ((), ()))


def product(a_high, a_low, b_high, b_low, dims):
    def dot(a, b):
        return lax.dot_general(a, b, dims, preferred_element_type=F32)

    return dot(a_high, b_high) + (dot(a_high, b_low) + dot(a_low, b_high))


def newton_kernel(
    full, vectors_ref, codes_ref, rotation_ref, sums_ref,
    whole, a_high, a_low, h, h_high, h_low, t_high, t_low, weights,
):
    y = lax.axis_index("dim")
    rows = vectors_ref.shape[1]

    square = jnp.zeros((8, 128), F32)
    for block in range(NY * NX * NC):
        for t in range(TILES):
            i, j = t // 6, t % 6
            tile = full[block, t]
            square = square + tile * tile
            whole[block * 24 + i * 8 : block * 24 + i * 8 + 8, j * 128 : j * 128 + 128] = tile
    magnitude = jnp.sqrt(jnp.sum(square))
    strips = [pl.ds(s * 256, 256) for s in range(3)]
    for strip in strips:
        a_high[strip], a_low[strip] = split(whole[strip] / magnitude)

    shape = (OWN, D)
    pick = lax.broadcasted_iota(jnp.int32, shape, 0) + y * OWN
    pick = jnp.where(pick == lax.broadcasted_iota(jnp.int32, shape, 1), 1.0, 0.0).astype(BF16)
    own = lax.dot_general(pick, a_high[...], NT, preferred_element_type=F32)
    own = own + lax.dot_general(pick, a_low[...], NT, preferred_element_type=F32)

    for strip in strips:
        value = product(a_high[strip], a_low[strip], a_high[...], a_low[...], NT)
        h[strip] = value
        h_high[strip], h_low[strip] = split(value)

    def times_h(value):
        high, low = split(value)
        return product(high, low, h_high[...], h_low[...], NN)

    for step in range(2):
        own = 1.5 * own - 0.5 * times_h(own)
        for strip in strips:
            value = product(h_high[strip], h_low[strip], h_high[...], h_low[...], NN)
            value = 1.5 * h[strip] - 0.5 * value
            whole[strip] = value
            t_high[strip], t_low[strip] = split(value)
        for strip in strips:
            value = product(t_high[strip], t_low[strip], h_high[...], h_low[...], NN)
            h[strip] = 1.5 * whole[strip] - 0.5 * value
        for strip in strips:
            h_high[strip], h_low[strip] = split(h[strip])
    own = 1.5 * own - 0.5 * times_h(own)
    last = times_h(own)
    for _ in range(2):
        last = 1.5 * last - 0.5 * times_h(last)
    own = 1.5 * own - 0.5 * last
    rotation_ref[...] = own

    rotated = jnp.dot(own.astype(BF16), vectors_ref[...], preferred_element_type=F32)
    rotated = rotated.astype(BF16).astype(F32)
    weights[:, :OWN] = rotated.T.astype(BF16)
    weights[:, OWN:] = jnp.where(
        lax.broadcasted_iota(jnp.int32, (rows, K - OWN), 1) < OWN_M, 1.0, 0.0
    ).astype(BF16)
    level = lax.broadcasted_iota(jnp.int32, (K, rows), 0)
    column = lax.broadcasted_iota(jnp.int32, (K, K), 1)
    subspace = jnp.where(column < OWN, column // SUB, column - OWN)
    total = jnp.zeros((K, K), F32)
    for m in range(OWN_M):
        onehot = jnp.where(level == codes_ref[m : m + 1, :], 1.0, 0.0).astype(BF16)
        value = jnp.dot(onehot, weights[...], preferred_element_type=F32)
        total = jnp.where(subspace == m, value, total)
    sums_ref[...] = total


def newton_and_sums(full, vectors_all, codes):
    rows = codes.shape[1]
    vmem = pl.BlockSpec(memory_space=pltpu.VMEM)
    square = (D, D)
    return pl.pallas_call(
        newton_kernel,
        out_shape=(
            jax.ShapeDtypeStruct((OWN, D), F32),
            jax.ShapeDtypeStruct((K, K), F32),
        ),
        in_specs=[vmem] * 3,
        out_specs=(vmem, vmem),
        scratch_shapes=[pltpu.VMEM(square, F32)]
        + [pltpu.VMEM(square, BF16)] * 2
        + [pltpu.VMEM(square, F32)]
        + [pltpu.VMEM(square, BF16)] * 4
        + [pltpu.VMEM((rows, K), BF16)],
        compiler_params=pltpu.CompilerParams(vmem_limit_bytes=50 * 2**20),
        name="newton_and_sums",
    )(full, vectors_all, codes)


def refit_kernel(sums_ref, book_ref, box_x, sum_x, box_z, mine, box_core, send_sem, recv_sem):
    x, z, core, y = position()
    sibling = device(x, z, 1 - core, y)
    across_x = [device(lax.rem(x + off, NX), z, core, y) for off in range(1, NX)]
    across_z = [device(x, lax.rem(z + off, NZ), core, y) for off in range(1, NZ)]
    greet([sibling] + across_x + across_z)
    sent = []

    def send(src, dst, k, peer):
        copy = remote(src, dst, send_sem, recv_sem, k, peer)
        copy.start()
        sent.append(copy)
        return copy

    stage = [
        send(sums_ref.at[lax.rem(x + i + 1, NX)], box_x.at[i], i, peer)
        for i, peer in enumerate(across_x)
    ]
    for copy in stage:
        copy.wait_recv()
    sum_x[...] = (sums_ref[x] + box_x[0]) + (box_x[1] + box_x[2])
    stage = [
        send(sum_x.at[lax.rem(z + i + 1, NZ)], box_z.at[i], 3 + i, peer)
        for i, peer in enumerate(across_z)
    ]
    for copy in stage:
        copy.wait_recv()
    total = sum_x[z]
    for i in range(NZ - 1):
        total = total + box_z[i]
    mine[...] = total
    send(mine, box_core, 10, sibling).wait_recv()
    book_ref[...] = mine[...] + box_core[...]
    for copy in sent:
        copy.wait_send()


def refit(sums):
    vmem = pl.BlockSpec(memory_space=pltpu.VMEM)
    return pl.pallas_call(
        refit_kernel,
        out_shape=jax.ShapeDtypeStruct((8, K), F32),
        in_specs=[vmem],
        out_specs=vmem,
        scratch_shapes=[
            pltpu.VMEM((NX - 1, NZ, 8, K), F32),
            pltpu.VMEM((NZ, 8, K), F32),
            pltpu.VMEM((NZ - 1, 8, K), F32),
            pltpu.VMEM((8, K), F32),
            pltpu.VMEM((8, K), F32),
            pltpu.SemaphoreType.DMA((11,)),
            pltpu.SemaphoreType.DMA((11,)),
        ],
        compiler_params=pltpu.CompilerParams(collective_id=2, has_side_effects=True),
        name="refit",
    )(sums)


def per_device(vectors, codes, codebook):
    rows = vectors.shape[1]
    codes_all, book_all = gather_codes(codes.astype(BF16), codebook.T)
    part = cross_part(codes_all.reshape(M, rows), book_all.reshape(D, K), vectors)
    full, vectors_all = sum_and_gather(
        part.reshape(NX, NC, PADDED, 8, 128), vectors
    )
    rotation, sums = newton_and_sums(
        full.reshape(NY * NX * NC, PADDED, 8, 128), vectors_all.reshape(D, rows), codes
    )
    pair = refit(sums.reshape(NX, NZ, 8, K))
    core = lax.rem(lax.axis_index("dp"), NC)
    mine = lax.dynamic_slice_in_dim(pair, core * (K // (NX * NZ * NC)), K // (NX * NZ * NC), 0)
    divisor = jnp.repeat(jnp.maximum(mine[:, OWN : OWN + OWN_M], 1.0), SUB, axis=1)
    return (rotation, mine[:, :OWN] / divisor)


def solution(mesh):
    placed = (P("dim", "dp"), P("dim", "dp"), P(None, "dim"))
    return jax.shard_map(
        per_device,
        mesh=mesh,
        in_specs=placed,
        out_specs=(P("dim", None), P("dp", "dim")),
        check_vma=False,
    )
```

time: 975 us -> 116 us (0.12)
  waiting for transfers between devices: 638 us -> 0 us
  blocking collectives: 245 us -> 0 us
  Pallas kernels: 0 us -> 106 us
  matrix products: 29.4 us -> 0 us
  local copies, waits for them, and re-layouts: 29.5 us -> 5.39 us
  between operations: 16 us -> 0.7 us
    all_gather x5 -> x0, waiting for transfers between devices: 458 us -> none  [the longest x4 424 us: gather_spread(): return lax.all_gather(rows, ('dp', 'dim'), axis=0, tiled=True)]
    unnamed x1 -> x0, blocking collectives: 245 us -> none
    unnamed x6 -> x0, waiting for transfers between devices: 180 us -> none
    pallas_call x0 -> x5, Pallas kernels: none -> 106 us  [the longest x1 44.2 us: sum_and_gather(): pl.pallas_call(sum_kernel, out_shape=(jax.ShapeDtypeStruct((NY, NX, NC, P...]
    dot_general x16 -> x0, matrix products: 29.4 us -> none  [the longest x4 8.47 us: newton_update(): gram_rows = jnp.dot(rows, whole.T, precision=lax.Precision.HIGHEST)]
    while x19 -> x0, local copies, waits for them, and re-layouts: 11.5 us -> none
  transfers between devices with their start and end apart: 7 -> 0, of which waited for: 6 -> 0; matrix products, arithmetic and copies ran while one was open for 0% -> 0% of each run, Pallas kernels for 0% -> 0%
where the time goes in v1:
time: 116 us
  Pallas kernels  106 us (91%)
  local copies, waits for them, and re-layouts  5.39 us (5%)
  other arithmetic  3.58 us (3%)
    pallas_call x1, Pallas kernels, sum_and_gather(): pl.pallas_call(sum_kernel, out_shape=(jax.ShapeDtypeStruct((NY, NX, NC, P...  44.2 us
    pallas_call x1, Pallas kernels, newton_and_sums(): pl.pallas_call(newton_kernel, out_shape=(jax.ShapeDtypeStruct((OWN, D), F...  26.2 us
    pallas_call x1, Pallas kernels, refit(): pl.pallas_call(refit_kernel, out_shape=jax.ShapeDtypeStruct((8, K), F32),...  17.2 us
    pallas_call x1, Pallas kernels, gather_codes(): pl.pallas_call(gather_kernel, out_shape=(jax.ShapeDtypeStruct((NY,) + cod...  11.8 us
    pallas_call x1, Pallas kernels, cross_part(): pl.pallas_call(cross_kernel, out_shape=jax.ShapeDtypeStruct((NX * NC, PAD...  6.93 us
    unnamed x12, local copies, waits for them, and re-layouts  5.22 us

profile of v1, /device:TPU:1, one launch (start us, length us, event | category | flops | bytes accessed | tf_op | source)
XLA Modules:
  0.0 116.0 jit_solution(11351357298926079648)
XLA Ops:
  0.6 0.0 copy-start.3
  0.6 1.5 %convert_element_type.3.codes_ref = bf16[16,1024]{1,0:T(8,128)(2,1)} convert(s32[16,1024]{1,0:T(8,128)} %codes_ref.1) | non-fusion elementwise | flops 16384 | bytes 98304 | tf_op jit(solution)/shard_map/convert_element_type | solution.py:421
  2.2 11.8 %gather_codes.1 = (bf16[4,16,1024]{2,1,0:T(8,128)(2,1)}, bf16[4,192,256]{2,1,0:T(8,128)(2,1)}) custom-call(bf16[16,1024]{1,0:T(8,128)(2,1)} %convert_element_type.3.codes_ref, bf16[192,256]{1,0:T(8,128)(2,1)} %bitcast.13), custom_call_target="tpu_custom_call" | custom-call | tf_op jit(solution)/shard_map/gather_codes/pallas_call | solution.py:72
  13.9 0.0 copy-start.1
  13.9 1.0 copy-done.1
  14.9 0.0 copy-start.2
  14.9 1.0 copy-done.2
  15.9 0.0 copy-start.5
  15.9 0.9 copy-done.5
  16.8 6.9 %cross_part.1 = f32[8,24,8,128]{3,2,1,0:T(8,128)S(1)} custom-call(bf16[64,1024]{1,0:T(8,128)(2,1)S(1)} %bitcast.12, bf16[768,256]{1,0:T(8,128)(2,1)S(1)} %bitcast.10, bf16[192,1024]{1,0:T(8,128)(2,1)S(1)} %copy-done.1), custom_call_target="tpu_custom_call" | custom-call | tf_op jit(solution)/shard_map/cross_part/pallas_call | solution.py:130
  23.8 44.2 %sum_and_gather.1 = (f32[4,4,2,24,8,128]{5,4,3,2,1,0:T(8,128)S(1)}, bf16[4,192,1024]{2,1,0:T(8,128)(2,1)S(1)}) custom-call(f32[4,2,24,8,128]{4,3,2,1,0:T(8,128)S(1)} %bitcast.8, bf16[192,1024]{1,0:T(8,128)(2,1)S(1)} %copy-done.1), custom_call_target="tpu_custom_call" | custom-call | tf_op jit(solution)/shard_map/sum_and_gather/pallas_call | solution.py:227
  68.0 0.0 copy-start
  68.0 1.6 %copy-done = f32[4,4,2,24,8,128]{5,4,3,2,1,0:T(8,128)} copy-done((f32[4,4,2,24,8,128]{5,4,3,2,1,0:T(8,128)}, f32[4,4,2,24,8,128]{5,4,3,2,1,0:T(8,128)S(1)}, u32[]{:S(2)}) %copy-start) | copy-done | bytes 3145752
  69.6 0.0 copy-done.3
  69.6 26.2 %newton_and_sums.1 = (f32[192,768]{1,0:T(8,128)}, f32[256,256]{1,0:T(8,128)S(1)}) custom-call(f32[32,24,8,128]{3,2,1,0:T(8,128)} %bitcast.7, bf16[768,1024]{1,0:T(8,128)(2,1)S(1)} %bitcast.9, s32[16,1024]{1,0:T(8,128)S(1)} %copy-done.3), custom_call_target="tpu_custom_call" | custom-call | tf_op jit(solution)/shard_map/newton_and_sums/pallas_call | solution.py:343
  95.9 0.0 copy-start.4
  95.9 0.7 copy-done.4
  96.5 17.2 %refit.1 = f32[8,256]{1,0:T(8,128)} custom-call(f32[4,8,8,256]{3,2,1,0:T(8,128)} %bitcast.11), custom_call_target="tpu_custom_call" | custom-call | tf_op jit(solution)/shard_map/refit/pallas_call | solution.py:400
  113.7 0.8 dynamic-slice_maximum_fusion
  114.5 0.1 broadcast_in_dim.3
  114.6 0.1 reshape.31
  114.7 1.3 %dynamic-slice_divide_fusion = f32[4,192]{1,0:T(4,128)} fusion(f32[4,192]{1,0:T(4,128)S(1)} %reshape.31, f32[8,256]{1,0:T(8,128)} %refit.1, s32[]{:T(128)S(6)} %select_n.3), kind=kLoop, calls=%fused_computation | loop fusion | flops 768 | bytes 9220 | tf_op jit(solution)/shard_map/div | solution.py:433
Async XLA Ops:
  0.6 69.0 %copy-start.3 = (s32[16,1024]{1,0:T(8,128)S(1)}, s32[16,1024]{1,0:T(8,128)}, u32[]{:S(2)}) copy-start(s32[16,1024]{1,0:T(8,128)} %codes_ref.1) | copy-start | bytes 196612
  13.9 1.0 copy-start.1
  14.9 1.0 copy-start.2
  15.9 0.9 copy-start.5
  68.0 1.6 %copy-start = (f32[4,4,2,24,8,128]{5,4,3,2,1,0:T(8,128)}, f32[4,4,2,24,8,128]{5,4,3,2,1,0:T(8,128)S(1)}, u32[]{:S(2)}) copy-start(f32[4,4,2,24,8,128]{5,4,3,2,1,0:T(8,128)S(1)} %get-tuple-element.10) | copy-start | bytes 9437188
  95.9 0.7 copy-start.4

commit v2 on v0

v2 whole, which is shorter than its diff:
```python
import jax
import jax.numpy as jnp
from jax import lax
from jax.experimental import pallas as pl
from jax.experimental.pallas import tpu as pltpu
from jax.sharding import PartitionSpec as P

NX, NZ, NC, NY = 4, 8, 2, 4
D, M, K = 768, 64, 256
SUB = D // M
OWN = D // NY
OWN_M = M // NY
TILES = 18
PER_Z = 3
HALF = TILES // 2
ROWS_K = K // NX // NC
MESH = pl.DeviceIdType.MESH
F32, BF16 = jnp.float32, jnp.bfloat16
NT = (((1,), (1,)), ((), ()))
NN = (((1,), (0,)), ((), ()))


def dot(a, b, dims):
    return lax.dot_general(a, b, dims, preferred_element_type=F32)


def split(value):
    high = value.astype(BF16)
    return high, (value - high.astype(F32)).astype(BF16)


def product(a_high, a_low, b_high, b_low, dims):
    return dot(a_high, b_high, dims) + (dot(a_high, b_low, dims) + dot(a_low, b_high, dims))


def position():
    dp = lax.axis_index("dp")
    y = lax.axis_index("dim")
    core = lax.rem(dp, NC)
    z = lax.rem(dp // NC, NZ)
    x = dp // (NC * NZ)
    return x, z, core, y


def device(x, z, core, y):
    return ((x * NZ + z) * NC + core, y)


def own_rows(y):
    return pl.ds(pl.multiple_of(y * OWN, 64), OWN)


def decode(codes_all, book_all, decoded, y):
    group = OWN_M // 2
    height = group * SUB
    rows = decoded.shape[1]
    which = lax.broadcasted_iota(jnp.int32, (height, 128), 0) // SUB
    for g in range(2):
        book = book_all[y, g * height : (g + 1) * height, :].astype(F32)
        low, high = book[:, :128], book[:, 128:]
        base = pl.multiple_of(y * OWN + g * height, 32)
        for block in range(rows // 128):
            cols = pl.ds(block * 128, 128)
            lines = codes_all[y, :, cols].astype(F32).astype(jnp.int32)
            index = jnp.broadcast_to(lines[g * group : g * group + 1], (height, 128))
            for s in range(1, group):
                line = lines[g * group + s : g * group + s + 1]
                index = jnp.where(which == s, jnp.broadcast_to(line, (height, 128)), index)
            lane = index & 127
            picked = jnp.where(
                index >= 128,
                jnp.take_along_axis(high, lane, axis=1),
                jnp.take_along_axis(low, lane, axis=1),
            )
            decoded[pl.ds(base, height), cols] = picked.astype(BF16)


def newton(y, whole, a_high, a_low, h, h_high, h_low, t_high, t_low):
    square = jnp.zeros((8, 128), F32)
    for s in range(D // 8):
        for j in range(D // 128):
            tile = whole[s * 8 : s * 8 + 8, j * 128 : j * 128 + 128]
            square = square + tile * tile
    energy = jnp.sum(square)
    side = 256
    count = D // side

    def cut(i):
        return slice(i * side, i * side + side)

    for i in range(count):
        a_high[cut(i)], a_low[cut(i)] = split(whole[cut(i)])

    shape = (OWN, D)
    pick = lax.broadcasted_iota(jnp.int32, shape, 0) + y * OWN
    pick = jnp.where(pick == lax.broadcasted_iota(jnp.int32, shape, 1), 1.0, 0.0).astype(BF16)
    own = dot(pick, a_high[...], NT) + dot(pick, a_low[...], NT)
    own = own / jnp.sqrt(energy)

    upper = [(i, j) for i in range(count) for j in range(i, count)]

    def put(full, high, low, i, j, value):
        full[cut(i), cut(j)] = value
        high[cut(i), cut(j)], low[cut(i), cut(j)] = split(value)
        if i != j:
            high[cut(j), cut(i)], low[cut(j), cut(i)] = split(value.T)

    def times_h(value):
        high, low = split(value)
        return product(high, low, h_high[...], h_low[...], NN)

    for i, j in upper:
        value = product(a_high[cut(i)], a_low[cut(i)], a_high[cut(j)], a_low[cut(j)], NT)
        put(h, h_high, h_low, i, j, value / energy)
    for step in range(2):
        own = 1.5 * own - 0.5 * times_h(own)
        for i, j in upper:
            value = product(h_high[cut(i)], h_low[cut(i)], h_high[:, cut(j)], h_low[:, cut(j)], NN)
            put(whole, t_high, t_low, i, j, 1.5 * h[cut(i), cut(j)] - 0.5 * value)
        for i, j in upper:
            value = product(t_high[cut(i)], t_low[cut(i)], h_high[:, cut(j)], h_low[:, cut(j)], NN)
            h[cut(i), cut(j)] = 1.5 * whole[cut(i), cut(j)] - 0.5 * value
        for i, j in upper:
            put(h, h_high, h_low, i, j, h[cut(i), cut(j)])
    own = 1.5 * own - 0.5 * times_h(own)
    last = times_h(own)
    for _ in range(2):
        last = 1.5 * last - 0.5 * times_h(last)
    return 1.5 * own - 0.5 * last


def kernel(
    vectors_ref, codes_ref, book_ref, rotation_ref, refit_ref,
    codes_all, book_all, vectors_all, decoded, part, box_core, sum_core, box_x, sum_x, box_z,
    full, whole, a_high, a_low, h, h_high, h_low, t_high, t_low,
    onehot, weights, sums, box_one, stage_two, box_two, send_sem, recv_sem,
):
    x, z, core, y = position()
    rows = vectors_ref.shape[1]
    sibling = device(x, z, 1 - core, y)
    across_x = [device(lax.rem(x + off, NX), z, core, y) for off in range(1, NX)]
    across_z = [device(x, lax.rem(z + off, NZ), core, y) for off in range(1, NZ)]
    across_y = [device(x, z, core, lax.rem(y + off, NY)) for off in range(1, NY)]
    other_x = [
        device(lax.rem(x + off, NX), z, 1 - core, y) for off in range(1, NX)
    ]
    sent = []
    number = [0]

    def send(src, dst, peer):
        k = number[0]
        number[0] += 1
        copy = pltpu.make_async_remote_copy(
            src_ref=src, dst_ref=dst, send_sem=send_sem.at[k], recv_sem=recv_sem.at[k],
            device_id=peer, device_id_type=MESH,
        )
        copy.start()
        sent.append(copy)
        return copy

    def spread(ref, peers):
        return [send(ref, ref, peer) for peer in peers]

    barrier = pltpu.get_barrier_semaphore()
    peers = [sibling] + across_x + other_x + across_z + across_y
    for peer in peers:
        pl.semaphore_signal(barrier, inc=1, device_id=peer, device_id_type=MESH)
    codes_all[y] = codes_ref[...].astype(F32).astype(BF16)
    book_all[y] = book_ref[...]
    sum_x[TILES:] = jnp.zeros((PER_Z * NZ - TILES, 8, 128), F32)
    stage_two[...] = jnp.zeros((NZ, 8, K), F32)
    weights[OWN:, :] = jnp.where(
        lax.broadcasted_iota(jnp.int32, (K - OWN, rows), 0) < OWN_M, 1.0, 0.0
    ).astype(BF16)
    pl.semaphore_wait(barrier, len(peers))

    arrivals = []
    for peer in across_y:
        arrivals.append(spread(codes_all.at[y], [peer]) + spread(book_all.at[y], [peer]))
    vectors_all[own_rows(y), :] = vectors_ref[...]
    decode(codes_all, book_all, decoded, y)
    for i, copies in enumerate(arrivals):
        for copy in copies:
            copy.wait_recv()
        decode(codes_all, book_all, decoded, lax.rem(y + NY - 1 - i, NY))
    mine = vectors_all.at[own_rows(y), :]
    vectors_here = spread(mine, across_y)

    value = dot(vectors_ref[...], decoded[...], NT)
    for pair in range(NX * NC):
        for t in range(TILES):
            i, j = pair * 3 + t // 6, t % 6
            part[pair // NC, pair % NC, t] = value[i * 8 : i * 8 + 8, j * 128 : j * 128 + 128]

    order = [lax.rem(x + off, NX) for off in (1, 2, 3, 0)]
    first = [send(part.at[i, 1 - core], box_core.at[i], sibling) for i in order]
    stage = []
    for n, copy in enumerate(first):
        i = order[n]
        copy.wait_recv()
        sum_core[i] = part[i, core] + box_core[i]
        if n < NX - 1:
            stage.append(send(sum_core.at[i], box_x.at[n], across_x[n]))
    place = lax.broadcasted_iota(jnp.int32, (K, rows), 0)
    level = ((place // 64) * 16 + (place // 4) % NZ * 2 + (place // 32) % NC) * 4 + place % 4
    for m in range(OWN_M):
        onehot[m * K : m * K + K] = jnp.where(level == codes_ref[m : m + 1, :], 1.0, 0.0).astype(BF16)
    for copy in stage:
        copy.wait_recv()
    sum_x[:TILES] = (sum_core[x] + box_x[0]) + (box_x[1] + box_x[2])
    stage = [
        send(sum_x.at[pl.ds(lax.rem(z + i + 1, NZ) * PER_Z, PER_Z)], box_z.at[i], peer)
        for i, peer in enumerate(across_z)
    ]
    for copy in stage:
        copy.wait_recv()
    share = pl.ds(z * PER_Z, PER_Z)
    total = sum_x[share]
    for i in range(NZ - 1):
        total = total + box_z[i]
    full[y, x, core, share] = total

    for copy in spread(full.at[y, x, core, share], across_z):
        copy.wait_recv()

    def piece(y, x, core, half):
        return full.at[y, x, core, pl.ds(half * HALF, HALF)]

    def lay(y, x, core, half):
        base = ((y * NX + x) * NC + core) * 24
        for t in range(half * HALF, half * HALF + HALF):
            row = pl.multiple_of(base + t // 6 * 8, 8)
            col = t % 6 * 128
            whole[pl.ds(row, 8), col : col + 128] = full[y, x, core, t]

    def before(index, off, size):
        return lax.rem(index + size - off, size)

    one, two = piece(y, x, core, 0), piece(y, x, core, 1)
    one_x, two_y = spread(one, across_x), spread(two, across_y)
    one_y, two_x = [spread(one, across_y)], [spread(two, across_x)]
    siblings = [(spread(one, [sibling])[0], y, x, 0), (spread(two, [sibling])[0], y, x, 1)]
    lay(y, x, core, 0)
    lay(y, x, core, 1)
    for i in range(NX - 1):
        from_x = before(x, i + 1, NX)
        one_x[i].wait_recv()
        ref = piece(y, from_x, core, 0)
        one_y.append(spread(ref, across_y))
        siblings.append((spread(ref, [sibling])[0], y, from_x, 0))
        from_y = before(y, i + 1, NY)
        two_y[i].wait_recv()
        ref = piece(from_y, x, core, 1)
        two_x.append(spread(ref, across_x))
        siblings.append((spread(ref, [sibling])[0], from_y, x, 1))
        lay(y, from_x, core, 0)
        lay(from_y, x, core, 1)
    for n in range(NX):
        for i in range(NX - 1):
            at_x, at_y = before(x, n, NX), before(y, i + 1, NY)
            one_y[n][i].wait_recv()
            siblings.append((spread(piece(at_y, at_x, core, 0), [sibling])[0], at_y, at_x, 0))
            lay(at_y, at_x, core, 0)
            at_x, at_y = before(x, i + 1, NX), before(y, n, NY)
            two_x[n][i].wait_recv()
            siblings.append((spread(piece(at_y, at_x, core, 1), [sibling])[0], at_y, at_x, 1))
            lay(at_y, at_x, core, 1)
    for copy, at_y, at_x, half in siblings:
        copy.wait_recv()
        lay(at_y, at_x, 1 - core, half)

    rotation = newton(y, whole, a_high, a_low, h, h_high, h_low, t_high, t_low)
    rotation_ref[...] = rotation

    for copy in vectors_here:
        copy.wait_recv()
    rotated = dot(rotation.astype(BF16), vectors_all[...], NN)
    weights[:OWN, :] = rotated.astype(BF16)
    column = lax.broadcasted_iota(jnp.int32, (K, K), 1)
    subspace = jnp.where(column < OWN, column // SUB, column - OWN)
    total = jnp.zeros((K, K), F32)
    for m in range(OWN_M):
        value = dot(onehot[m * K : m * K + K], weights[...], NT)
        total = jnp.where(subspace == m, value, total)
    for i in range(NX * NC):
        sums[i] = total[i * ROWS_K : (i + 1) * ROWS_K]

    stage = []
    for peers, core_to in ((across_x, core), ([sibling] + other_x, 1 - core)):
        for i, peer in enumerate(peers):
            off = i + 1 if len(peers) == NX - 1 else i
            target = lax.rem(x + off, NX) * NC + core_to
            stage.append(send(sums.at[target], box_one.at[len(stage)], peer))
    for copy in stage:
        copy.wait_recv()
    total = sums[x * NC + core]
    for i in range(len(stage)):
        total = total + box_one[i]
    for i in range(NZ):
        stage_two[i, 0:4] = total[i * 4 : i * 4 + 4]
    stage = [
        send(stage_two.at[lax.rem(z + i + 1, NZ)], box_two.at[i], peer)
        for i, peer in enumerate(across_z)
    ]
    for copy in stage:
        copy.wait_recv()
    total = stage_two[z]
    for i in range(NZ - 1):
        total = total + box_two[i]
    left, right = total[:, :128], total[:, 128:]
    lane = lax.broadcasted_iota(jnp.int32, (8, 128), 1)
    offset = OWN - 128
    count = jnp.take_along_axis(right, offset + lane // SUB, axis=1)
    refit_ref[:, :128] = (left / jnp.maximum(count, 1.0))[0:4]
    count = jnp.take_along_axis(right, offset + jnp.minimum((lane + 128) // SUB, OWN_M - 1), axis=1)
    refit_ref[:, 128:] = (right / jnp.maximum(count, 1.0))[0:4, :offset]
    for copy in sent:
        copy.wait_send()


def per_device(vectors, codes, codebook):
    rows = vectors.shape[1]
    vmem = pl.BlockSpec(memory_space=pltpu.VMEM)
    square = (D, D)
    copies = 6 + 3 + 4 + 3 + 7 + 7 + 12 + 2 + 24 + 24 + 7 + 7
    rotation, refit = pl.pallas_call(
        kernel,
        out_shape=(
            jax.ShapeDtypeStruct((OWN, D), F32),
            jax.ShapeDtypeStruct((K // (NX * NZ * NC), OWN), F32),
        ),
        in_specs=[vmem] * 3,
        out_specs=(vmem, vmem),
        scratch_shapes=[
            pltpu.VMEM((NY, OWN_M, rows), BF16),
            pltpu.VMEM((NY, OWN, K), BF16),
            pltpu.VMEM((D, rows), BF16),
            pltpu.VMEM((D, rows), BF16),
            pltpu.VMEM((NX, NC, TILES, 8, 128), F32),
            pltpu.VMEM((NX, TILES, 8, 128), F32),
            pltpu.VMEM((NX, TILES, 8, 128), F32),
            pltpu.VMEM((NX - 1, TILES, 8, 128), F32),
            pltpu.VMEM((PER_Z * NZ, 8, 128), F32),
            pltpu.VMEM((NZ - 1, PER_Z, 8, 128), F32),
            pltpu.VMEM((NY, NX, NC, PER_Z * NZ, 8, 128), F32),
            pltpu.VMEM(square, F32),
            pltpu.VMEM(square, BF16),
            pltpu.VMEM(square, BF16),
            pltpu.VMEM(square, F32),
            pltpu.VMEM(square, BF16),
            pltpu.VMEM(square, BF16),
            pltpu.VMEM(square, BF16),
            pltpu.VMEM(square, BF16),
            pltpu.VMEM((OWN_M * K, rows), BF16),
            pltpu.VMEM((K, rows), BF16),
            pltpu.VMEM((NX * NC, ROWS_K, K), F32),
            pltpu.VMEM((NX * NC - 1, ROWS_K, K), F32),
            pltpu.VMEM((NZ, 8, K), F32),
            pltpu.VMEM((NZ - 1, 8, K), F32),
            pltpu.SemaphoreType.DMA((copies,)),
            pltpu.SemaphoreType.DMA((copies,)),
        ],
        compiler_params=pltpu.CompilerParams(
            collective_id=0, has_side_effects=True, vmem_limit_bytes=56 * 2**20
        ),
        name="rotate_and_refit",
    )(vectors, codes, codebook.T)
    return rotation, refit


def solution(mesh):
    placed = (P("dim", "dp"), P("dim", "dp"), P(None, "dim"))
    return jax.shard_map(
        per_device,
        mesh=mesh,
        in_specs=placed,
        out_specs=(P("dim", None), P("dp", "dim")),
        check_vma=False,
    )
```

time: 975 us -> 85.1 us (0.09)
  waiting for transfers between devices: 638 us -> 0 us
  blocking collectives: 245 us -> 0 us
  Pallas kernels: 0 us -> 81.9 us
  matrix products: 29.4 us -> 0 us
  local copies, waits for them, and re-layouts: 29.5 us -> 2.51 us
  between operations: 16 us -> 0.65 us
  other arithmetic: 10.7 us -> 0 us
    all_gather x5 -> x0, waiting for transfers between devices: 458 us -> none  [the longest x4 424 us: gather_spread(): return lax.all_gather(rows, ('dp', 'dim'), axis=0, tiled=True)]
    unnamed x1 -> x0, blocking collectives: 245 us -> none
    unnamed x6 -> x0, waiting for transfers between devices: 180 us -> none
    pallas_call x0 -> x1, Pallas kernels: none -> 81.9 us  [per_device(): pl.pallas_call(kernel, out_shape=(jax.ShapeDtypeStruct((OWN, D), F32), ja...]
    dot_general x16 -> x0, matrix products: 29.4 us -> none  [the longest x4 8.47 us: newton_update(): gram_rows = jnp.dot(rows, whole.T, precision=lax.Precision.HIGHEST)]
    while x19 -> x0, local copies, waits for them, and re-layouts: 11.5 us -> none
  transfers between devices with their start and end apart: 7 -> 0, of which waited for: 6 -> 0; matrix products, arithmetic and copies ran while one was open for 0% -> 0% of each run, Pallas kernels for 0% -> 0%
where the time goes in v2:
time: 85.1 us; the launch traced here: 85 us
  Pallas kernels  81.9 us (96%)
  local copies, waits for them, and re-layouts  2.51 us (3%)
    pallas_call x1, Pallas kernels, per_device(): pl.pallas_call(kernel, out_shape=(jax.ShapeDtypeStruct((OWN, D), F32), ja...  81.9 us
    unnamed x4, local copies, waits for them, and re-layouts  2.51 us

profile of v2, /device:TPU:1, one launch (start us, length us, event | category | flops | bytes accessed | tf_op | source)
XLA Modules:
  0.0 85.0 jit_solution(17745270053470080948)
XLA Ops:
  0.6 81.9 %rotate_and_refit.1 = (f32[192,768]{1,0:T(8,128)}, f32[4,192]{1,0:T(4,128)}) custom-call(bf16[192,1024]{1,0:T(8,128)(2,1)} %vectors_ref.1, s32[16,1024]{1,0:T(8,128)} %codes_ref.1, bf16[192,256]{1,0:T(8,128)(2,1)} %bitcast.1), custom_call_target="tpu_custom_call" | custom-call | tf_op jit(solution)/shard_map/rotate_and_refit/pallas_call | solution.py:326
  82.5 0.0 copy-start
  82.5 1.9 %copy.7 = f32[192,768]{1,0:T(8,128)} copy(f32[192,768]{1,0:T(8,128)} %get-tuple-element.4) | data formatting | bytes 1179648
  84.4 0.0 copy-done
  84.4 0.6 copy.8
Async XLA Ops:
  82.5 1.9 %copy-start = (f32[4,192]{1,0:T(4,128)S(1)}, f32[4,192]{1,0:T(4,128)}, u32[]{:S(2)}) copy-start(f32[4,192]{1,0:T(4,128)} %get-tuple-element.5) | copy-start | bytes 9220

commit v3 on v2

--- a/solution.py
+++ b/solution.py
@@ -76,12 +76,14 @@
 
 
 def newton(y, whole, a_high, a_low, h, h_high, h_low, t_high, t_low):
-    square = jnp.zeros((8, 128), F32)
+    squares = [jnp.zeros((8, 128), F32)] * 12
     for s in range(D // 8):
         for j in range(D // 128):
             tile = whole[s * 8 : s * 8 + 8, j * 128 : j * 128 + 128]
-            square = square + tile * tile
-    energy = jnp.sum(square)
+            n = s % 2 * 6 + j
+            squares[n] = squares[n] + tile * tile
+    energy = jnp.sum(sum(squares[1:], squares[0]))
+    scale = 1.0 / energy
     side = 256
     count = D // side
 
@@ -91,11 +93,10 @@
     for i in range(count):
         a_high[cut(i)], a_low[cut(i)] = split(whole[cut(i)])
 
-    shape = (OWN, D)
-    pick = lax.broadcasted_iota(jnp.int32, shape, 0) + y * OWN
-    pick = jnp.where(pick == lax.broadcasted_iota(jnp.int32, shape, 1), 1.0, 0.0).astype(BF16)
-    own = dot(pick, a_high[...], NT) + dot(pick, a_low[...], NT)
-    own = own / jnp.sqrt(energy)
+    start = pl.multiple_of(y * OWN - 64 * lax.rem(y, 2), 128)
+    own = whole[:, pl.ds(start, 256)]
+    own = jnp.where(lax.rem(y, 2) == 1, pltpu.roll(own, 192, 1), own)
+    own = own.T[:OWN] / jnp.sqrt(energy)
 
     upper = [(i, j) for i in range(count) for j in range(i, count)]
 
@@ -111,7 +112,7 @@
 
     for i, j in upper:
         value = product(a_high[cut(i)], a_low[cut(i)], a_high[cut(j)], a_low[cut(j)], NT)
-        put(h, h_high, h_low, i, j, value / energy)
+        put(h, h_high, h_low, i, j, value * scale)
     for step in range(2):
         own = 1.5 * own - 0.5 * times_h(own)
         for i, j in upper:
@@ -130,13 +131,13 @@
 
 
 def kernel(
-    vectors_ref, codes_ref, book_ref, rotation_ref, refit_ref,
-    codes_all, book_all, vectors_all, decoded, part, box_core, sum_core, box_x, sum_x, box_z,
+    vectors_hbm, codes_hbm, book_hbm, rotation_hbm, refit_ref,
+    codes_ref, rotation_ref, codes_all, book_all, vectors_all, decoded, part, box_core, sum_core, box_x, sum_x, box_z,
     full, whole, a_high, a_low, h, h_high, h_low, t_high, t_low,
-    onehot, weights, sums, box_one, stage_two, box_two, send_sem, recv_sem,
+    onehot, weights, sums, box_one, stage_two, box_two, send_sem, recv_sem, local_sem,
 ):
     x, z, core, y = position()
-    rows = vectors_ref.shape[1]
+    rows = vectors_all.shape[1]
     sibling = device(x, z, 1 - core, y)
     across_x = [device(lax.rem(x + off, NX), z, core, y) for off in range(1, NX)]
     across_z = [device(x, lax.rem(z + off, NZ), core, y) for off in range(1, NZ)]
@@ -165,28 +166,34 @@
     peers = [sibling] + across_x + other_x + across_z + across_y
     for peer in peers:
         pl.semaphore_signal(barrier, inc=1, device_id=peer, device_id_type=MESH)
-    codes_all[y] = codes_ref[...].astype(F32).astype(BF16)
-    book_all[y] = book_ref[...]
+    mine = vectors_all.at[own_rows(y), :]
+    load_codes = pltpu.make_async_copy(codes_hbm, codes_ref, local_sem.at[0])
+    load_book = pltpu.make_async_copy(book_hbm, book_all.at[y], local_sem.at[1])
+    load_vectors = pltpu.make_async_copy(vectors_hbm, mine, local_sem.at[2])
+    for copy in (load_codes, load_book, load_vectors):
+        copy.start()
     sum_x[TILES:] = jnp.zeros((PER_Z * NZ - TILES, 8, 128), F32)
     stage_two[...] = jnp.zeros((NZ, 8, K), F32)
     weights[OWN:, :] = jnp.where(
         lax.broadcasted_iota(jnp.int32, (K - OWN, rows), 0) < OWN_M, 1.0, 0.0
     ).astype(BF16)
+    load_codes.wait()
+    codes_all[y] = codes_ref[...].astype(F32).astype(BF16)
+    load_book.wait()
+    load_vectors.wait()
     pl.semaphore_wait(barrier, len(peers))
 
     arrivals = []
     for peer in across_y:
         arrivals.append(spread(codes_all.at[y], [peer]) + spread(book_all.at[y], [peer]))
-    vectors_all[own_rows(y), :] = vectors_ref[...]
     decode(codes_all, book_all, decoded, y)
     for i, copies in enumerate(arrivals):
         for copy in copies:
             copy.wait_recv()
         decode(codes_all, book_all, decoded, lax.rem(y + NY - 1 - i, NY))
-    mine = vectors_all.at[own_rows(y), :]
     vectors_here = spread(mine, across_y)
 
-    value = dot(vectors_ref[...], decoded[...], NT)
+    value = dot(vectors_all[own_rows(y), :], decoded[...], NT)
     for pair in range(NX * NC):
         for t in range(TILES):
             i, j = pair * 3 + t // 6, t % 6
@@ -201,10 +208,14 @@
         sum_core[i] = part[i, core] + box_core[i]
         if n < NX - 1:
             stage.append(send(sum_core.at[i], box_x.at[n], across_x[n]))
-    place = lax.broadcasted_iota(jnp.int32, (K, rows), 0)
-    level = ((place // 64) * 16 + (place // 4) % NZ * 2 + (place // 32) % NC) * 4 + place % 4
+    place = lax.broadcasted_iota(jnp.int32, (ROWS_K, rows), 0)
+    level = place // 4 * 8 + place % 4
     for m in range(OWN_M):
-        onehot[m * K : m * K + K] = jnp.where(level == codes_ref[m : m + 1, :], 1.0, 0.0).astype(BF16)
+        code = jnp.broadcast_to(codes_ref[m : m + 1, :], (ROWS_K, rows))
+        for chunk in range(NX * NC):
+            at = (chunk * OWN_M + m) * ROWS_K
+            same = level == code - (chunk // NC * 64 + chunk % NC * 4)
+            onehot[at : at + ROWS_K] = jnp.where(same, 1.0, 0.0).astype(BF16)
     for copy in stage:
         copy.wait_recv()
     sum_x[:TILES] = (sum_core[x] + box_x[0]) + (box_x[1] + box_x[2])
@@ -271,29 +282,31 @@
 
     rotation = newton(y, whole, a_high, a_low, h, h_high, h_low, t_high, t_low)
     rotation_ref[...] = rotation
+    store_rotation = pltpu.make_async_copy(rotation_ref, rotation_hbm, local_sem.at[3])
+    store_rotation.start()
 
     for copy in vectors_here:
         copy.wait_recv()
     rotated = dot(rotation.astype(BF16), vectors_all[...], NN)
     weights[:OWN, :] = rotated.astype(BF16)
-    column = lax.broadcasted_iota(jnp.int32, (K, K), 1)
+    column = lax.broadcasted_iota(jnp.int32, (ROWS_K, K), 1)
     subspace = jnp.where(column < OWN, column // SUB, column - OWN)
-    total = jnp.zeros((K, K), F32)
-    for m in range(OWN_M):
-        value = dot(onehot[m * K : m * K + K], weights[...], NT)
-        total = jnp.where(subspace == m, value, total)
-    for i in range(NX * NC):
-        sums[i] = total[i * ROWS_K : (i + 1) * ROWS_K]
 
     stage = []
-    for peers, core_to in ((across_x, core), ([sibling] + other_x, 1 - core)):
-        for i, peer in enumerate(peers):
-            off = i + 1 if len(peers) == NX - 1 else i
-            target = lax.rem(x + off, NX) * NC + core_to
-            stage.append(send(sums.at[target], box_one.at[len(stage)], peer))
+    height = OWN_M * ROWS_K
+    for n, (off, flip) in enumerate(((2, 0), (2, 1), (1, 0), (1, 1), (3, 0), (3, 1), (0, 1), (0, 0))):
+        to_x, to_core = lax.rem(x + off, NX), lax.rem(core + flip, NC)
+        chunk = pl.multiple_of((to_x * NC + to_core) * height, height)
+        value = dot(onehot[pl.ds(chunk, height)], weights[...], NT)
+        total = jnp.zeros((ROWS_K, K), F32)
+        for m in range(OWN_M):
+            total = jnp.where(subspace == m, value[m * ROWS_K : (m + 1) * ROWS_K], total)
+        sums[n] = total
+        if n < NX * NC - 1:
+            stage.append(send(sums.at[n], box_one.at[n], device(to_x, z, to_core, y)))
     for copy in stage:
         copy.wait_recv()
-    total = sums[x * NC + core]
+    total = sums[NX * NC - 1]
     for i in range(len(stage)):
         total = total + box_one[i]
     for i in range(NZ):
@@ -316,11 +329,13 @@
     refit_ref[:, 128:] = (right / jnp.maximum(count, 1.0))[0:4, :offset]
     for copy in sent:
         copy.wait_send()
+    store_rotation.wait()
 
 
 def per_device(vectors, codes, codebook):
     rows = vectors.shape[1]
     vmem = pl.BlockSpec(memory_space=pltpu.VMEM)
+    anywhere = pl.BlockSpec(memory_space=pl.ANY)
     square = (D, D)
     copies = 6 + 3 + 4 + 3 + 7 + 7 + 12 + 2 + 24 + 24 + 7 + 7
     rotation, refit = pl.pallas_call(
@@ -329,9 +344,11 @@
             jax.ShapeDtypeStruct((OWN, D), F32),
             jax.ShapeDtypeStruct((K // (NX * NZ * NC), OWN), F32),
         ),
-        in_specs=[vmem] * 3,
-        out_specs=(vmem, vmem),
+        in_specs=[anywhere] * 3,
+        out_specs=(anywhere, vmem),
         scratch_shapes=[
+            pltpu.VMEM((OWN_M, rows), jnp.int32),
+            pltpu.VMEM((OWN, D), F32),
             pltpu.VMEM((NY, OWN_M, rows), BF16),
             pltpu.VMEM((NY, OWN, K), BF16),
             pltpu.VMEM((D, rows), BF16),
@@ -359,6 +376,7 @@
             pltpu.VMEM((NZ - 1, 8, K), F32),
             pltpu.SemaphoreType.DMA((copies,)),
             pltpu.SemaphoreType.DMA((copies,)),
+            pltpu.SemaphoreType.DMA((4,)),
         ],
         compiler_params=pltpu.CompilerParams(
             collective_id=0, has_side_effects=True, vmem_limit_bytes=56 * 2**20

time: 85.1 us -> 81.9 us (0.962)
  Pallas kernels: 81.9 us -> 78.6 us
    pallas_call x1, Pallas kernels: 81.9 us -> 78.6 us  [per_device(): pl.pallas_call(kernel, out_shape=(jax.ShapeDtypeStruct((OWN, D), F32), ja...]
where the time goes in v3:
time: 81.9 us; the launch traced here: 81.7 us
  Pallas kernels  78.6 us (96%)
  local copies, waits for them, and re-layouts  2.51 us (3%)
    pallas_call x1, Pallas kernels, per_device(): pl.pallas_call(kernel, out_shape=(jax.ShapeDtypeStruct((OWN, D), F32), ja...  78.6 us
    unnamed x4, local copies, waits for them, and re-layouts  2.51 us

profile of v3, /device:TPU:1, one launch (start us, length us, event | category | flops | bytes accessed | tf_op | source)
XLA Modules:
  0.0 81.7 jit_solution(18152597512065029860)
XLA Ops:
  0.6 78.6 %rotate_and_refit.1 = (f32[192,768]{1,0:T(8,128)}, f32[4,192]{1,0:T(4,128)}) custom-call(bf16[192,1024]{1,0:T(8,128)(2,1)} %vectors_hbm.1, s32[16,1024]{1,0:T(8,128)} %codes_hbm.1, bf16[192,256]{1,0:T(8,128)(2,1)} %bitcast.1), custom_call_target="tpu_custom_call" | custom-call | tf_op jit(solution)/shard_map/rotate_and_refit/pallas_call | solution.py:341
  79.2 0.0 copy-start
  79.2 1.9 %copy.7 = f32[192,768]{1,0:T(8,128)} copy(f32[192,768]{1,0:T(8,128)} %get-tuple-element.4) | data formatting | bytes 1179648
  81.1 0.0 copy-done
  81.1 0.6 copy.8
Async XLA Ops:
  79.2 1.9 %copy-start = (f32[4,192]{1,0:T(4,128)S(1)}, f32[4,192]{1,0:T(4,128)}, u32[]{:S(2)}) copy-start(f32[4,192]{1,0:T(4,128)} %get-tuple-element.5) | copy-start | bytes 9220

commit v4 on v3

--- a/solution.py
+++ b/solution.py
@@ -50,29 +50,29 @@
     return pl.ds(pl.multiple_of(y * OWN, 64), OWN)
 
 
-def decode(codes_all, book_all, decoded, y):
+def decode(codes_all, book_all, decoded, y, half):
     group = OWN_M // 2
     height = group * SUB
     rows = decoded.shape[1]
     which = lax.broadcasted_iota(jnp.int32, (height, 128), 0) // SUB
-    for g in range(2):
-        book = book_all[y, g * height : (g + 1) * height, :].astype(F32)
-        low, high = book[:, :128], book[:, 128:]
-        base = pl.multiple_of(y * OWN + g * height, 32)
-        for block in range(rows // 128):
-            cols = pl.ds(block * 128, 128)
-            lines = codes_all[y, :, cols].astype(F32).astype(jnp.int32)
-            index = jnp.broadcast_to(lines[g * group : g * group + 1], (height, 128))
-            for s in range(1, group):
-                line = lines[g * group + s : g * group + s + 1]
-                index = jnp.where(which == s, jnp.broadcast_to(line, (height, 128)), index)
-            lane = index & 127
-            picked = jnp.where(
-                index >= 128,
-                jnp.take_along_axis(high, lane, axis=1),
-                jnp.take_along_axis(low, lane, axis=1),
-            )
-            decoded[pl.ds(base, height), cols] = picked.astype(BF16)
+    book = book_all[y, half].astype(F32)
+    low, high = book[:, :128], book[:, 128:]
+    base = pl.multiple_of(y * OWN + half * height, 32)
+    for block in range(rows // 128):
+        cols = pl.ds(block * 128, 128)
+        both = codes_all[y, :, cols].astype(F32).astype(jnp.int32)
+        lines = jnp.where(half == 0, both[:group], both[group:])
+        index = jnp.broadcast_to(lines[0:1], (height, 128))
+        for s in range(1, group):
+            line = jnp.broadcast_to(lines[s : s + 1], (height, 128))
+            index = jnp.where(which == s, line, index)
+        lane = index & 127
+        picked = jnp.where(
+            index >= 128,
+            jnp.take_along_axis(high, lane, axis=1),
+            jnp.take_along_axis(low, lane, axis=1),
+        )
+        decoded[pl.ds(base, height), cols] = picked.astype(BF16)
 
 
 def newton(y, whole, a_high, a_low, h, h_high, h_low, t_high, t_low):
@@ -172,7 +172,6 @@
     load_vectors = pltpu.make_async_copy(vectors_hbm, mine, local_sem.at[2])
     for copy in (load_codes, load_book, load_vectors):
         copy.start()
-    sum_x[TILES:] = jnp.zeros((PER_Z * NZ - TILES, 8, 128), F32)
     stage_two[...] = jnp.zeros((NZ, 8, K), F32)
     weights[OWN:, :] = jnp.where(
         lax.broadcasted_iota(jnp.int32, (K - OWN, rows), 0) < OWN_M, 1.0, 0.0
@@ -185,12 +184,19 @@
 
     arrivals = []
     for peer in across_y:
-        arrivals.append(spread(codes_all.at[y], [peer]) + spread(book_all.at[y], [peer]))
-    decode(codes_all, book_all, decoded, y)
-    for i, copies in enumerate(arrivals):
-        for copy in copies:
-            copy.wait_recv()
-        decode(codes_all, book_all, decoded, lax.rem(y + NY - 1 - i, NY))
+        arrivals += spread(codes_all.at[y], [peer]) + spread(book_all.at[y, core], [peer])
+    decode(codes_all, book_all, decoded, y, core)
+    decode(codes_all, book_all, decoded, y, 1 - core)
+    sources = [lax.rem(y + NY - 1 - i, NY) for i in range(NY - 1)]
+    passed = []
+    for i, source in enumerate(sources):
+        arrivals[2 * i].wait_recv()
+        arrivals[2 * i + 1].wait_recv()
+        passed += spread(book_all.at[source, core], [sibling])
+        decode(codes_all, book_all, decoded, source, core)
+    for i, source in enumerate(sources):
+        passed[i].wait_recv()
+        decode(codes_all, book_all, decoded, source, 1 - core)
     vectors_here = spread(mine, across_y)
 
     value = dot(vectors_all[own_rows(y), :], decoded[...], NT)
@@ -219,20 +225,47 @@
     for copy in stage:
         copy.wait_recv()
     sum_x[:TILES] = (sum_core[x] + box_x[0]) + (box_x[1] + box_x[2])
-    stage = [
-        send(sum_x.at[pl.ds(lax.rem(z + i + 1, NZ) * PER_Z, PER_Z)], box_z.at[i], peer)
-        for i, peer in enumerate(across_z)
-    ]
-    for copy in stage:
-        copy.wait_recv()
+    shared = TILES // PER_Z
+    first_z = number[0]
+    number[0] += 2 * (NZ - 1)
+
+    def along_z(k, src, dst, i):
+        return pltpu.make_async_remote_copy(
+            src_ref=src, dst_ref=dst,
+            send_sem=send_sem.at[first_z + k], recv_sem=recv_sem.at[first_z + k],
+            device_id=across_z[i], device_id_type=MESH,
+        )
+
+    def part_copy(i):
+        share = pl.ds(lax.rem(z + i + 1, NZ) * PER_Z, PER_Z)
+        return along_z(i, sum_x.at[share], box_z.at[i], i)
+
     share = pl.ds(z * PER_Z, PER_Z)
-    total = sum_x[share]
+
+    def total_copy(i):
+        own = full.at[y, x, core, share]
+        return along_z(NZ - 1 + i, own, own, i)
+
     for i in range(NZ - 1):
-        total = total + box_z[i]
-    full[y, x, core, share] = total
-
-    for copy in spread(full.at[y, x, core, share], across_z):
-        copy.wait_recv()
+        @pl.when(lax.rem(z + i + 1, NZ) < shared)
+        def _():
+            part_copy(i).start()
+
+    @pl.when(z < shared)
+    def _():
+        for i in range(NZ - 1):
+            part_copy(i).wait_recv()
+        total = sum_x[share]
+        for i in range(NZ - 1):
+            total = total + box_z[i]
+        full[y, x, core, share] = total
+        for i in range(NZ - 1):
+            total_copy(i).start()
+
+    for i in range(NZ - 1):
+        @pl.when(lax.rem(z + NZ - i - 1, NZ) < shared)
+        def _():
+            total_copy(i).wait_recv()
 
     def piece(y, x, core, half):
         return full.at[y, x, core, pl.ds(half * HALF, HALF)]
@@ -320,6 +353,22 @@
     total = stage_two[z]
     for i in range(NZ - 1):
         total = total + box_two[i]
+    refit_ref[...] = total
+    for copy in sent:
+        copy.wait_send()
+    for i in range(NZ - 1):
+        @pl.when(lax.rem(z + i + 1, NZ) < shared)
+        def _():
+            part_copy(i).wait_send()
+        @pl.when(z < shared)
+        def _():
+            total_copy(i).wait_send()
+    store_rotation.wait()
+
+
+def finish_kernel(rotation_ref, totals_ref, out_ref, refit_ref):
+    out_ref[...] = rotation_ref[...]
+    total = totals_ref[...]
     left, right = total[:, :128], total[:, 128:]
     lane = lax.broadcasted_iota(jnp.int32, (8, 128), 1)
     offset = OWN - 128
@@ -327,9 +376,6 @@
     refit_ref[:, :128] = (left / jnp.maximum(count, 1.0))[0:4]
     count = jnp.take_along_axis(right, offset + jnp.minimum((lane + 128) // SUB, OWN_M - 1), axis=1)
     refit_ref[:, 128:] = (right / jnp.maximum(count, 1.0))[0:4, :offset]
-    for copy in sent:
-        copy.wait_send()
-    store_rotation.wait()
 
 
 def per_device(vectors, codes, codebook):
@@ -337,12 +383,12 @@
     vmem = pl.BlockSpec(memory_space=pltpu.VMEM)
     anywhere = pl.BlockSpec(memory_space=pl.ANY)
     square = (D, D)
-    copies = 6 + 3 + 4 + 3 + 7 + 7 + 12 + 2 + 24 + 24 + 7 + 7
-    rotation, refit = pl.pallas_call(
+    copies = 9 + 3 + 4 + 3 + 7 + 7 + 12 + 2 + 24 + 24 + 7 + 7
+    rotation, totals = pl.pallas_call(
         kernel,
         out_shape=(
             jax.ShapeDtypeStruct((OWN, D), F32),
-            jax.ShapeDtypeStruct((K // (NX * NZ * NC), OWN), F32),
+            jax.ShapeDtypeStruct((8, K), F32),
         ),
         in_specs=[anywhere] * 3,
         out_specs=(anywhere, vmem),
@@ -350,7 +396,7 @@
             pltpu.VMEM((OWN_M, rows), jnp.int32),
             pltpu.VMEM((OWN, D), F32),
             pltpu.VMEM((NY, OWN_M, rows), BF16),
-            pltpu.VMEM((NY, OWN, K), BF16),
+            pltpu.VMEM((NY, 2, OWN // 2, K), BF16),
             pltpu.VMEM((D, rows), BF16),
             pltpu.VMEM((D, rows), BF16),
             pltpu.VMEM((NX, NC, TILES, 8, 128), F32),
@@ -382,8 +428,17 @@
             collective_id=0, has_side_effects=True, vmem_limit_bytes=56 * 2**20
         ),
         name="rotate_and_refit",
-    )(vectors, codes, codebook.T)
-    return rotation, refit
+    )(vectors, codes, codebook.T.reshape(2, OWN // 2, K))
+    return pl.pallas_call(
+        finish_kernel,
+        out_shape=(
+            jax.ShapeDtypeStruct((OWN, D), F32),
+            jax.ShapeDtypeStruct((K // (NX * NZ * NC), OWN), F32),
+        ),
+        in_specs=[vmem, vmem],
+        out_specs=(vmem, vmem),
+        name="finish",
+    )(rotation, totals)
 
 
 def solution(mesh):

time: 81.9 us -> 78.8 us (0.962)
  local copies, waits for them, and re-layouts: 2.51 us -> 0 us
    unnamed x4 -> x0, local copies, waits for them, and re-layouts: 2.51 us -> none
    pallas_call x1, Pallas kernels: 78.6 us -> 76.1 us  [per_device(): pl.pallas_call(kernel, out_shape=(jax.ShapeDtypeStruct((OWN, D), F32), ja...]
    pallas_call x0 -> x1, Pallas kernels: none -> 1.92 us  [per_device(): pl.pallas_call(finish_kernel, out_shape=(jax.ShapeDtypeStruct((OWN, D), F...]
where the time goes in v4:
time: 78.8 us; the launch traced here: 78.7 us
  Pallas kernels  78.1 us (99%)
    pallas_call x1, Pallas kernels, per_device(): pl.pallas_call(kernel, out_shape=(jax.ShapeDtypeStruct((OWN, D), F32), ja...  76.1 us
    pallas_call x1, Pallas kernels, per_device(): pl.pallas_call(finish_kernel, out_shape=(jax.ShapeDtypeStruct((OWN, D), F...  1.92 us

profile of v4, /device:TPU:1, one launch (start us, length us, event | category | flops | bytes accessed | tf_op | source)
XLA Modules:
  0.0 78.7 jit_solution(10791984832233398930)
XLA Ops:
  0.6 76.1 %rotate_and_refit.1 = (f32[192,768]{1,0:T(8,128)}, f32[8,256]{1,0:T(8,128)}) custom-call(bf16[192,1024]{1,0:T(8,128)(2,1)} %vectors_hbm.1, s32[16,1024]{1,0:T(8,128)} %codes_hbm.1, bf16[2,96,256]{2,1,0:T(8,128)(2,1)} %bitcast.3), custom_call_target="tpu_custom_call" | custom-call | tf_op jit(solution)/shard_map/rotate_and_refit/pallas_call | solution.py:387
  76.8 1.9 %finish.1 = (f32[192,768]{1,0:T(8,128)}, f32[4,192]{1,0:T(4,128)}) custom-call(f32[192,768]{1,0:T(8,128)} %get-tuple-element.4.rotation_ref, f32[8,256]{1,0:T(8,128)} %get-tuple-element.5.totals_ref), custom_call_target="tpu_custom_call" | custom-call | tf_op jit(solution)/shard_map/finish/pallas_call | solution.py:432

commit v5 on v4

--- a/solution.py
+++ b/solution.py
@@ -14,6 +14,8 @@
 PER_Z = 3
 HALF = TILES // 2
 ROWS_K = K // NX // NC
+FOUR = (2, 1, 3)
+EIGHT = (4, 3, 5, 2, 6, 1, 7)
 MESH = pl.DeviceIdType.MESH
 F32, BF16 = jnp.float32, jnp.bfloat16
 NT = (((1,), (1,)), ((), ()))
@@ -139,9 +141,9 @@
     x, z, core, y = position()
     rows = vectors_all.shape[1]
     sibling = device(x, z, 1 - core, y)
-    across_x = [device(lax.rem(x + off, NX), z, core, y) for off in range(1, NX)]
-    across_z = [device(x, lax.rem(z + off, NZ), core, y) for off in range(1, NZ)]
-    across_y = [device(x, z, core, lax.rem(y + off, NY)) for off in range(1, NY)]
+    across_x = [device(lax.rem(x + off, NX), z, core, y) for off in FOUR]
+    across_z = [device(x, lax.rem(z + off, NZ), core, y) for off in EIGHT]
+    across_y = [device(x, z, core, lax.rem(y + off, NY)) for off in FOUR]
     other_x = [
         device(lax.rem(x + off, NX), z, 1 - core, y) for off in range(1, NX)
     ]
@@ -187,7 +189,7 @@
         arrivals += spread(codes_all.at[y], [peer]) + spread(book_all.at[y, core], [peer])
     decode(codes_all, book_all, decoded, y, core)
     decode(codes_all, book_all, decoded, y, 1 - core)
-    sources = [lax.rem(y + NY - 1 - i, NY) for i in range(NY - 1)]
+    sources = [lax.rem(y + NY - off, NY) for off in FOUR]
     passed = []
     for i, source in enumerate(sources):
         arrivals[2 * i].wait_recv()
@@ -205,7 +207,7 @@
             i, j = pair * 3 + t // 6, t % 6
             part[pair // NC, pair % NC, t] = value[i * 8 : i * 8 + 8, j * 128 : j * 128 + 128]
 
-    order = [lax.rem(x + off, NX) for off in (1, 2, 3, 0)]
+    order = [lax.rem(x + off, NX) for off in FOUR + (0,)]
     first = [send(part.at[i, 1 - core], box_core.at[i], sibling) for i in order]
     stage = []
     for n, copy in enumerate(first):
@@ -237,7 +239,7 @@
         )
 
     def part_copy(i):
-        share = pl.ds(lax.rem(z + i + 1, NZ) * PER_Z, PER_Z)
+        share = pl.ds(lax.rem(z + EIGHT[i], NZ) * PER_Z, PER_Z)
         return along_z(i, sum_x.at[share], box_z.at[i], i)
 
     share = pl.ds(z * PER_Z, PER_Z)
@@ -247,7 +249,7 @@
         return along_z(NZ - 1 + i, own, own, i)
 
     for i in range(NZ - 1):
-        @pl.when(lax.rem(z + i + 1, NZ) < shared)
+        @pl.when(lax.rem(z + EIGHT[i], NZ) < shared)
         def _():
             part_copy(i).start()
 
@@ -263,7 +265,7 @@
             total_copy(i).start()
 
     for i in range(NZ - 1):
-        @pl.when(lax.rem(z + NZ - i - 1, NZ) < shared)
+        @pl.when(lax.rem(z + NZ - EIGHT[i], NZ) < shared)
         def _():
             total_copy(i).wait_recv()
 
@@ -279,6 +281,8 @@
 
     def before(index, off, size):
         return lax.rem(index + size - off, size)
+
+    steps = (0,) + FOUR
 
     one, two = piece(y, x, core, 0), piece(y, x, core, 1)
     one_x, two_y = spread(one, across_x), spread(two, across_y)
@@ -287,12 +291,12 @@
     lay(y, x, core, 0)
     lay(y, x, core, 1)
     for i in range(NX - 1):
-        from_x = before(x, i + 1, NX)
+        from_x = before(x, FOUR[i], NX)
         one_x[i].wait_recv()
         ref = piece(y, from_x, core, 0)
         one_y.append(spread(ref, across_y))
         siblings.append((spread(ref, [sibling])[0], y, from_x, 0))
-        from_y = before(y, i + 1, NY)
+        from_y = before(y, FOUR[i], NY)
         two_y[i].wait_recv()
         ref = piece(from_y, x, core, 1)
         two_x.append(spread(ref, across_x))
@@ -301,11 +305,11 @@
         lay(from_y, x, core, 1)
     for n in range(NX):
         for i in range(NX - 1):
-            at_x, at_y = before(x, n, NX), before(y, i + 1, NY)
+            at_x, at_y = before(x, steps[n], NX), before(y, FOUR[i], NY)
             one_y[n][i].wait_recv()
             siblings.append((spread(piece(at_y, at_x, core, 0), [sibling])[0], at_y, at_x, 0))
             lay(at_y, at_x, core, 0)
-            at_x, at_y = before(x, i + 1, NX), before(y, n, NY)
+            at_x, at_y = before(x, FOUR[i], NX), before(y, steps[n], NY)
             two_x[n][i].wait_recv()
             siblings.append((spread(piece(at_y, at_x, core, 1), [sibling])[0], at_y, at_x, 1))
             lay(at_y, at_x, core, 1)
@@ -345,7 +349,7 @@
     for i in range(NZ):
         stage_two[i, 0:4] = total[i * 4 : i * 4 + 4]
     stage = [
-        send(stage_two.at[lax.rem(z + i + 1, NZ)], box_two.at[i], peer)
+        send(stage_two.at[lax.rem(z + EIGHT[i], NZ)], box_two.at[i], peer)
         for i, peer in enumerate(across_z)
     ]
     for copy in stage:
@@ -357,7 +361,7 @@
     for copy in sent:
         copy.wait_send()
     for i in range(NZ - 1):
-        @pl.when(lax.rem(z + i + 1, NZ) < shared)
+        @pl.when(lax.rem(z + EIGHT[i], NZ) < shared)
         def _():
             part_copy(i).wait_send()
         @pl.when(z < shared)

time: 78.8 us -> 76.3 us (0.968)
  Pallas kernels: 78.1 us -> 75.5 us
    pallas_call x1, Pallas kernels: 76.1 us -> 73.6 us  [per_device(): pl.pallas_call(kernel, out_shape=(jax.ShapeDtypeStruct((OWN, D), F32), ja...]
where the time goes in v5:
time: 76.3 us; the launch traced here: 76.2 us
  Pallas kernels  75.5 us (99%)
    pallas_call x1, Pallas kernels, per_device(): pl.pallas_call(kernel, out_shape=(jax.ShapeDtypeStruct((OWN, D), F32), ja...  73.6 us
    pallas_call x1, Pallas kernels, per_device(): pl.pallas_call(finish_kernel, out_shape=(jax.ShapeDtypeStruct((OWN, D), F...  1.92 us

profile of v5, /device:TPU:1, one launch (start us, length us, event | category | flops | bytes accessed | tf_op | source)
XLA Modules:
  0.0 76.2 jit_solution(1670498454507204895)
XLA Ops:
  0.6 73.6 %rotate_and_refit.1 = (f32[192,768]{1,0:T(8,128)}, f32[8,256]{1,0:T(8,128)}) custom-call(bf16[192,1024]{1,0:T(8,128)(2,1)} %vectors_hbm.1, s32[16,1024]{1,0:T(8,128)} %codes_hbm.1, bf16[2,96,256]{2,1,0:T(8,128)(2,1)} %bitcast.3), custom_call_target="tpu_custom_call" | custom-call | tf_op jit(solution)/shard_map/rotate_and_refit/pallas_call | solution.py:391
  74.3 1.9 %finish.1 = (f32[192,768]{1,0:T(8,128)}, f32[4,192]{1,0:T(4,128)}) custom-call(f32[192,768]{1,0:T(8,128)} %get-tuple-element.4.rotation_ref, f32[8,256]{1,0:T(8,128)} %get-tuple-element.5.totals_ref), custom_call_target="tpu_custom_call" | custom-call | tf_op jit(solution)/shard_map/finish/pallas_call | solution.py:436

commit v6 on v5

--- a/solution.py
+++ b/solution.py
@@ -110,7 +110,8 @@
 
     def times_h(value):
         high, low = split(value)
-        return product(high, low, h_high[...], h_low[...], NN)
+        both = dot(jnp.concatenate([high, low], axis=0), h_high[...], NN)
+        return both[:OWN] + (both[OWN:] + dot(high, h_low[...], NN))
 
     for i, j in upper:
         value = product(a_high[cut(i)], a_low[cut(i)], a_high[cut(j)], a_low[cut(j)], NT)
@@ -165,7 +166,7 @@
         return [send(ref, ref, peer) for peer in peers]
 
     barrier = pltpu.get_barrier_semaphore()
-    peers = [sibling] + across_x + other_x + across_z + across_y
+    peers = across_z + other_x + across_x + across_y + [sibling]
     for peer in peers:
         pl.semaphore_signal(barrier, inc=1, device_id=peer, device_id_type=MESH)
     mine = vectors_all.at[own_rows(y), :]

time: 76.3 us -> 75.9 us (level)
  no operation moved by 1% of the time
where the time goes in v6:
time: 75.9 us; the launch traced here: 75.8 us
  Pallas kernels  75.1 us (99%)
    pallas_call x1, Pallas kernels, per_device(): pl.pallas_call(kernel, out_shape=(jax.ShapeDtypeStruct((OWN, D), F32), ja...  73.2 us
    pallas_call x1, Pallas kernels, per_device(): pl.pallas_call(finish_kernel, out_shape=(jax.ShapeDtypeStruct((OWN, D), F...  1.92 us

profile of v6, /device:TPU:1, one launch (start us, length us, event | category | flops | bytes accessed | tf_op | source)
XLA Modules:
  0.0 75.8 jit_solution(7918356293673043944)
XLA Ops:
  0.6 73.2 %rotate_and_refit.1 = (f32[192,768]{1,0:T(8,128)}, f32[8,256]{1,0:T(8,128)}) custom-call(bf16[192,1024]{1,0:T(8,128)(2,1)} %vectors_hbm.1, s32[16,1024]{1,0:T(8,128)} %codes_hbm.1, bf16[2,96,256]{2,1,0:T(8,128)(2,1)} %bitcast.3), custom_call_target="tpu_custom_call" | custom-call | tf_op jit(solution)/shard_map/rotate_and_refit/pallas_call | solution.py:392
  73.8 1.9 %finish.1 = (f32[192,768]{1,0:T(8,128)}, f32[4,192]{1,0:T(4,128)}) custom-call(f32[192,768]{1,0:T(8,128)} %get-tuple-element.4.rotation_ref, f32[8,256]{1,0:T(8,128)} %get-tuple-element.5.totals_ref), custom_call_target="tpu_custom_call" | custom-call | tf_op jit(solution)/shard_map/finish/pallas_call | solution.py:437

commit v7 on v6

--- a/solution.py
+++ b/solution.py
@@ -265,10 +265,11 @@
         for i in range(NZ - 1):
             total_copy(i).start()
 
-    for i in range(NZ - 1):
-        @pl.when(lax.rem(z + NZ - EIGHT[i], NZ) < shared)
-        def _():
-            total_copy(i).wait_recv()
+    def await_half(half):
+        for i in range(NZ - 1):
+            @pl.when(lax.rem(z + NZ - EIGHT[i], NZ) // (shared // 2) == half)
+            def _():
+                total_copy(i).wait_recv()
 
     def piece(y, x, core, half):
         return full.at[y, x, core, pl.ds(half * HALF, HALF)]
@@ -286,7 +287,10 @@
     steps = (0,) + FOUR
 
     one, two = piece(y, x, core, 0), piece(y, x, core, 1)
-    one_x, two_y = spread(one, across_x), spread(two, across_y)
+    await_half(0)
+    one_x = spread(one, across_x)
+    await_half(1)
+    two_y = spread(two, across_y)
     one_y, two_x = [spread(one, across_y)], [spread(two, across_x)]
     siblings = [(spread(one, [sibling])[0], y, x, 0), (spread(two, [sibling])[0], y, x, 1)]
     lay(y, x, core, 0)

time: 75.9 us -> 75.8 us (level)
  no operation moved by 1% of the time
where the time goes in v7:
time: 75.8 us; the launch traced here: 75.7 us
  Pallas kernels  75 us (99%)
    pallas_call x1, Pallas kernels, per_device(): pl.pallas_call(kernel, out_shape=(jax.ShapeDtypeStruct((OWN, D), F32), ja...  73.1 us
    pallas_call x1, Pallas kernels, per_device(): pl.pallas_call(finish_kernel, out_shape=(jax.ShapeDtypeStruct((OWN, D), F...  1.92 us

profile of v7, /device:TPU:1, one launch (start us, length us, event | category | flops | bytes accessed | tf_op | source)
XLA Modules:
  0.0 75.7 jit_solution(6428100436646184528)
XLA Ops:
  0.6 73.1 %rotate_and_refit.1 = (f32[192,768]{1,0:T(8,128)}, f32[8,256]{1,0:T(8,128)}) custom-call(bf16[192,1024]{1,0:T(8,128)(2,1)} %vectors_hbm.1, s32[16,1024]{1,0:T(8,128)} %codes_hbm.1, bf16[2,96,256]{2,1,0:T(8,128)(2,1)} %bitcast.3), custom_call_target="tpu_custom_call" | custom-call | tf_op jit(solution)/shard_map/rotate_and_refit/pallas_call | solution.py:396
  73.8 1.9 %finish.1 = (f32[192,768]{1,0:T(8,128)}, f32[4,192]{1,0:T(4,128)}) custom-call(f32[192,768]{1,0:T(8,128)} %get-tuple-element.4.rotation_ref, f32[8,256]{1,0:T(8,128)} %get-tuple-element.5.totals_ref), custom_call_target="tpu_custom_call" | custom-call | tf_op jit(solution)/shard_map/finish/pallas_call | solution.py:441

commit v8 on v7

--- a/solution.py
+++ b/solution.py
@@ -289,11 +289,12 @@
     one, two = piece(y, x, core, 0), piece(y, x, core, 1)
     await_half(0)
     one_x = spread(one, across_x)
+    siblings = [(spread(one, [sibling])[0], y, x, 0)]
+    lay(y, x, core, 0)
     await_half(1)
     two_y = spread(two, across_y)
     one_y, two_x = [spread(one, across_y)], [spread(two, across_x)]
-    siblings = [(spread(one, [sibling])[0], y, x, 0), (spread(two, [sibling])[0], y, x, 1)]
-    lay(y, x, core, 0)
+    siblings.append((spread(two, [sibling])[0], y, x, 1))
     lay(y, x, core, 1)
     for i in range(NX - 1):
         from_x = before(x, FOUR[i], NX)

time: 75.8 us -> 75.8 us (level)
  no operation moved by 1% of the time
where the time goes in v8:
time: 75.8 us; the launch traced here: 75.7 us
  Pallas kernels  75 us (99%)
    pallas_call x1, Pallas kernels, per_device(): pl.pallas_call(kernel, out_shape=(jax.ShapeDtypeStruct((OWN, D), F32), ja...  73.1 us
    pallas_call x1, Pallas kernels, per_device(): pl.pallas_call(finish_kernel, out_shape=(jax.ShapeDtypeStruct((OWN, D), F...  1.92 us

profile of v8, /device:TPU:1, one launch (start us, length us, event | category | flops | bytes accessed | tf_op | source)
XLA Modules:
  0.0 75.7 jit_solution(3735140693770303010)
XLA Ops:
  0.6 73.1 %rotate_and_refit.1 = (f32[192,768]{1,0:T(8,128)}, f32[8,256]{1,0:T(8,128)}) custom-call(bf16[192,1024]{1,0:T(8,128)(2,1)} %vectors_hbm.1, s32[16,1024]{1,0:T(8,128)} %codes_hbm.1, bf16[2,96,256]{2,1,0:T(8,128)(2,1)} %bitcast.3), custom_call_target="tpu_custom_call" | custom-call | tf_op jit(solution)/shard_map/rotate_and_refit/pallas_call | solution.py:397
  73.7 1.9 %finish.1 = (f32[192,768]{1,0:T(8,128)}, f32[4,192]{1,0:T(4,128)}) custom-call(f32[192,768]{1,0:T(8,128)} %get-tuple-element.4.rotation_ref, f32[8,256]{1,0:T(8,128)} %get-tuple-element.5.totals_ref), custom_call_target="tpu_custom_call" | custom-call | tf_op jit(solution)/shard_map/finish/pallas_call | solution.py:442
